TPU v7x, 256 devices: a whole 4x4x8 slice. The times are simulated.
256 devices in a mesh: loop: 2 (over core), group: 2 (over x_lo), rep: 64 (over z, y, x_hi).
Axes of the slice: x: 4 (x_hi: 2, x_lo: 2; x = x_hi * 2 + x_lo), y: 4, z: 8, core: 2. Of those that a mesh axis runs over, the one named last changes fastest.
Arguments:
- frames: bfloat16 [512, 256, 128], P(('loop', 'rep'), 'group'), may hold values from -6 to 6
- factors: bfloat16 [128, 256, 128], P(None, ('loop', 'group')), as said below
- comp_means: bfloat16 [256, 128], P(('loop', 'group')), may hold values from -3 to 3
- log_weights: bfloat16 [256], P(('loop', 'group')), may hold values from -4 to 4
- pair_lists: int32 [512, 2, 2, 4], P(('loop', 'rep'), 'group'), may hold values from 0 to 3, as said below
- counts: int32 [512, 2, 2], P(('loop', 'rep'), 'group'), may hold values from 1 to 4
Outputs:
- occupancy: float32 [256], P(('loop', 'group'))
- first_moment: float32 [256, 128], P(('loop', 'group'))
- second_moment: float32 [128, 256, 128], P(None, ('loop', 'group'))
- frame_loglik: float32 [512, 256], P(('loop', 'rep'), 'group')
Inputs may be any that keep to these rules, and one draw needn't show every extreme that they name: Each pair_lists[b, g, l, :] is an ordering of the 4 blocks of that panel. `factors`: every factor is upper triangular with a positive diagonal.
All inputs are finite; a program needn't handle non-finite values.
Results may differ from a plain program's by a relative error of at most 0.002.
Values may be sent and summed in bfloat16 or wider, within the bound.
No kernel may reach another device: no remote copies, remote signals or barrier semaphores. Data moves between devices by JAX's collectives and lax.ppermute only.
A program may use at most 128 MiB of HBM per device.

v0:
```python
import math

import jax
import jax.numpy as jnp
from jax import lax
from jax.sharding import PartitionSpec as P

CB = 16


half_log = 0.5 * math.log(2.0 * math.pi)


def from_behind(value, axis, by):
    count = lax.axis_size(axis)
    return lax.ppermute(value, axis, [(i, (i + by) % count) for i in range(count)])


def combined_all(value, axis, join):
    pieces = jax.tree.map(lambda part: lax.all_gather(part, axis), value)
    head = jax.tree.map(lambda part: part[0], pieces)
    tail = jax.tree.map(lambda part: part[1:], pieces)
    so_far, _ = lax.scan(lambda so_far, piece: (join(so_far, piece), None), head, tail)
    return so_far


def score_panel(frame_rows, panel):
    factors, comp_means, log_weights = panel
    features = factors.shape[0]
    panel_size = factors.shape[1]
    centre = jnp.einsum("kd,dke->ke", comp_means, factors, preferred_element_type=jnp.float32)
    diagonal = jnp.einsum("iki->ki", factors).astype(jnp.float32)
    bias = (
        log_weights.astype(jnp.float32) + jnp.sum(jnp.log(diagonal), axis=1) - half_log * features
    )
    flat = factors.reshape(features, panel_size * features)
    pieces = []
    for offset_comp in range(0, panel_size, CB):
        product = jnp.dot(
            frame_rows,
            flat[:, offset_comp * features : (offset_comp + CB) * features],
            preferred_element_type=jnp.float32,
        )
        shifted = product.reshape(-1, CB, features) - centre[offset_comp : offset_comp + CB]
        pieces.append(jnp.sum(shifted * shifted, axis=-1))
    return bias - 0.5 * jnp.concatenate(pieces, axis=1)


def combine_partial(earlier, later):
    highest = jnp.maximum(earlier[0], later[0])
    return (
        highest,
        earlier[1] * jnp.exp(earlier[0] - highest) + later[1] * jnp.exp(later[0] - highest),
    )


def accumulate(carry, item):
    occupancy, first_moment, second_moment = carry
    weights, frame_block = item
    block_rows, panel_size = weights.shape
    features = frame_block.shape[1]
    weighted = (
        weights.astype(jnp.float32)[:, :, None] * frame_block.astype(jnp.float32)[:, None, :]
    ).astype(jnp.bfloat16)
    occupancy = occupancy + jnp.sum(weights.astype(jnp.float32), axis=0)
    first_moment = first_moment + jnp.sum(weighted.astype(jnp.float32), axis=0)
    second_moment = second_moment + lax.dot_general(
        frame_block,
        weighted.reshape(block_rows, panel_size * features),
        (((0,), (0,)), ((), ())),
        preferred_element_type=jnp.float32,
    )
    return ((occupancy, first_moment, second_moment), None)


def per_device(frames, factors, comp_means, log_weights, pair_lists, counts):
    loop_size = lax.axis_size("loop")
    blocks = frames.shape[0]
    own_rows = frames.shape[1]
    features = frames.shape[2]
    panel_size = factors.shape[1]
    gathered = lax.all_gather(frames, "group", axis=1, tiled=True)
    block_rows = gathered.shape[1]
    frame_rows = gathered.reshape(blocks * block_rows, features)
    panel = (factors, comp_means, log_weights)
    slot_index = jnp.arange(pair_lists.shape[3], dtype=jnp.int32)
    loop_index = lax.axis_index("loop")
    group_index = lax.axis_index("group")
    frames_in = lax.all_gather(gathered, "loop", axis=0, tiled=True)
    scores = {0: score_panel(frame_rows, panel)}
    current = panel
    current = from_behind((current[0], current[1], current[2]), "loop", 1)
    scores[1] = score_panel(frame_rows, current)
    stacked = jnp.stack([scores[offset] for offset in range(loop_size)])
    ordered = jnp.roll(stacked[::-1], loop_index + 1, axis=0).reshape(
        loop_size, blocks, block_rows, panel_size
    )
    in_use = slot_index[None, None, :] < counts[:, 0, :, None]
    hits = (pair_lists[:, 0, :, :, None] == slot_index[None, None, None, :]) & in_use[:, :, :, None]
    listed = jnp.any(hits, axis=2)
    allowed = jnp.transpose(jnp.repeat(listed, CB, axis=2), (1, 0, 2))[:, :, None, :]
    masked = jnp.where(allowed, ordered, -jnp.inf)
    highest = jnp.max(masked, axis=(0, 3))
    exp_total = jnp.sum(jnp.exp(masked - highest[None, :, :, None]), axis=(0, 3))
    highest, exp_total = combined_all((highest, exp_total), "group", combine_partial)
    loglik = highest + jnp.log(exp_total)
    frame_loglik = lax.dynamic_slice_in_dim(loglik, group_index * own_rows, own_rows, 1)
    weights = jnp.exp(masked - loglik[None, :, :, None]).astype(jnp.bfloat16)
    received = lax.all_to_all(weights, "loop", split_axis=0, concat_axis=1, tiled=True)
    weights_in = received.reshape(loop_size * blocks, block_rows, panel_size)
    initial = (
        jnp.zeros((panel_size,), jnp.float32),
        jnp.zeros((panel_size, features), jnp.float32),
        jnp.zeros((features, panel_size * features), jnp.float32),
    )
    (occupancy, first_moment, second_moment), unused = lax.scan(
        accumulate, initial, (weights_in, frames_in)
    )
    occupancy, first_moment, second_moment = lax.psum(
        (occupancy, first_moment, second_moment), "rep"
    )
    return (
        occupancy,
        first_moment,
        second_moment.reshape(features, panel_size, features),
        frame_loglik,
    )


def solution(mesh):
    return jax.shard_map(
        per_device,
        mesh=mesh,
        in_specs=(
            P(("loop", "rep"), "group", None),
            P(None, ("loop", "group"), None),
            P(("loop", "group"), None),
            P(("loop", "group")),
            P(("loop", "rep"), "group", None, None),
            P(("loop", "rep"), "group", None),
        ),
        out_specs=(
            P(("loop", "group")),
            P(("loop", "group"), None),
            P(None, ("loop", "group"), None),
            P(("loop", "rep"), "group"),
        ),
        check_vma=False,
    )
```

profile of v0, /device:TPU:4, one launch (start us, length us, event | category | flops | bytes accessed | tf_op | source)
XLA Modules:
  0.0 852.5 jit_solution(13724141577569043623)
XLA Ops:
  8.0 3.3 copy.59
  13.3 6.5 all_gather.18
  19.8 2.2 all_gather.23
  27.6 2.8 select_reduce_fusion.1
  30.5 3.5 copy.60
  41.5 4.4 all_gather.22
  45.8 4.3 all_gather.20
  50.5 3.9 all_to_all.4
  54.5 68.5 %while.4 = (s32[]{:T(128)}, f32[64]{0:T(128)S(1)}, f32[64,128]{1,0:T(8,128)S(1)}, f32[128,8192]{1,0:T(8,128)}, bf16[8,256,64]{1,2,0:T(8,128)(2,1)S(1)}, /*index=...) while((s32[]{:T(128)}, f32[64]{0:T(128)S(1)}, f32[64,128]{1,0:T(8,128)S(1)}, ...), condition=%wide.region_18.19_spmd.clone, body=%wide.region_15.18_spmd.clone.sunk | while | flops 547446848 | bytes 51184812 | solution.py:116
  54.7 3.3 multiply_convert_fusion.2
  58.0 3.0 convolution_add_fusion.2
  61.0 2.0 copy-done.1
  63.3 3.3 multiply_convert_fusion.2
  66.6 3.0 convolution_add_fusion.2
  71.8 3.3 multiply_convert_fusion.2
  75.1 3.0 convolution_add_fusion.2
  78.2 2.0 copy-done.1
  80.4 3.3 multiply_convert_fusion.2
  83.7 3.0 convolution_add_fusion.2
  89.0 3.3 multiply_convert_fusion.2
  92.3 3.0 convolution_add_fusion.2
  95.3 2.0 copy-done.1
  97.5 3.3 multiply_convert_fusion.2
  100.8 3.0 convolution_add_fusion.2
  106.1 3.3 multiply_convert_fusion.2
  109.4 3.0 convolution_add_fusion.2
  114.7 3.3 multiply_convert_fusion.2
  118.0 3.0 convolution_add_fusion.2
  123.0 4.9 copy.63
  127.9 354.5 %all-reduce = (f32[64]{0:T(128)}, f32[64,128]{1,0:T(8,128)}) all-reduce(f32[64]{0:T(128)S(1)} %get-tuple-element.53, f32[64,128]{1,0:T(8,128)S(1)} %get-tuple-element.54), channel_id=1, replica_groups=mesh['loop'=2,'group'=2,'rep'=64] {'rep'}, use_global_device_ids=true, to_apply=%region_19.20 | all-reduce | flops 8256 | bytes 66048 | tf_op jit(solution)/shard_map/psum | solution.py:119
  483.1 357.8 %all-reduce.3.cloned.1.call-done = f32[128,64,128]{2,1,0:T(8,128)} async-done(((f32[128,64,128]{2,1,0:T(8,128)}), f32[128,64,128]{2,1,0:T(8,128)}) %all-reduce.3.cloned.1.call-update) | async-done | bytes 4194320 | tf_op jit(solution)/shard_map/psum | solution.py:119
  840.9 4.8 copy.89
  (147 shorter events, 28.5 us)
Async XLA Ops:
  7.2 5.0 copy-start.4
  7.2 4.2 copy-start.6
  7.2 4.3 copy-start.5
  7.2 6.1 copy-start.3
  7.2 833.7 %all-reduce.3.cloned.1.call-start = ((), (), s32[]{:S(2)}) async-start(), calls=%async_computation.1 | async-start | bytes 8388608 | tf_op jit(solution)/shard_map/psum | solution.py:119
  7.3 33.4 %collective-permute-start = (bf16[64]{0:T(256)(128)(2,1)}, bf16[64]{0:T(256)(128)(2,1)S(1)}, u32[]{:S(2)}, u32[]{:S(2)}) collective-permute-start(bf16[64]{0:T(256)(128)(2,1)} %param.11), channel_id=1, source_target_pairs={{0,128},{128,0},{1,129},{129,1},{2,130},{130,2},{3,131},{131,3},{4... | collective-permute-start | bytes 392 | tf_op jit(solution)/shard_map/ppermute | solution.py:16
  7.4 26.6 %collective-permute-start.2 = (bf16[64,128]{1,0:T(8,128)(2,1)}, bf16[64,128]{1,0:T(8,128)(2,1)S(1)}, u32[]{:S(2)}, u32[]{:S(2)}) collective-permute-start(bf16[64,128]{1,0:T(8,128)(2,1)} %param.10), channel_id=1, source_target_pairs={{0,128},{128,0},{1,129},{129,1},{2,130},{130,2},{3,131},{131,3},{4... | collective-permute-start | bytes 49160 | tf_op jit(solution)/shard_map/ppermute | solution.py:16
  7.8 19.4 %collective-permute-start.1 = (bf16[128,64,128]{2,1,0:T(8,128)(2,1)}, bf16[128,64,128]{2,1,0:T(8,128)(2,1)}, u32[]{:S(2)}, u32[]{:S(2)}) collective-permute-start(bf16[128,64,128]{2,1,0:T(8,128)(2,1)} %param.9), channel_id=1, source_target_pairs={{0,128},{128,0},{1,129},{129,1},{2,130},{130,2},{3,131},{131,3},{4... | collective-permute-start | bytes 6291464 | tf_op jit(solution)/shard_map/ppermute | solution.py:16
  26.0 1.6 copy-start.2
  27.3 3.2 copy-start.7
  54.6 3.4 copy-start
  61.0 2.0 copy-start.1
  63.2 3.4 copy-start
  69.6 2.0 copy-start.1
  71.7 3.4 copy-start
  78.1 2.0 copy-start.1
  80.3 3.4 copy-start
  86.7 2.0 copy-start.1
  88.9 3.4 copy-start
  95.3 2.0 copy-start.1
  97.4 3.4 copy-start
  103.8 2.0 copy-start.1
  106.0 3.4 copy-start
  112.4 2.0 copy-start.1
  114.6 3.4 copy-start
  121.0 2.0 copy-start.1
Sparse Core Ops, SparseCore 0:
  128.0 712.7 all-reduce.2
where the time goes:
time: 856 us; the launch traced here: 853 us
  blocking collectives  376 us (44%)
  waiting for transfers between devices  358 us (42%)
  matrix products  36.5 us (4%)
  local copies, waits for them, and re-layouts  35.7 us (4%)
  other arithmetic  31 us (4%)
  between operations  14.4 us (2%)
    psum x1, waiting for transfers between devices, per_device(): lax.psum((occupancy, first_moment, second_moment), 'rep')  358 us
    psum x1, blocking collectives, per_device(): lax.psum((occupancy, first_moment, second_moment), 'rep')  355 us
    convert_element_type x8, other arithmetic, accumulate(): weighted = (weights.astype(jnp.float32)[:, :, None] * frame_block.astype(...  26.2 us
    dot_general x8, matrix products, accumulate(): lax.dot_general(frame_block, weighted.reshape(block_rows, panel_size * fe...  24 us
  transfers between devices with their start and end apart: 4, of which 1 were waited for; matrix products, arithmetic and copies ran while one was open for 3% of the time, Pallas kernels for 0%

commit v1 on v0

v1 whole, which is shorter than its diff:
```python
import functools
import math

import jax
import jax.numpy as jnp
from jax import lax
from jax.experimental import pallas as pl
from jax.experimental.pallas import tpu as pltpu
from jax.sharding import Mesh
from jax.sharding import PartitionSpec as P

D = 128
KC = 64
CB = 16
NF = 2048
SH = 512
ROWS = 72
HALF = 64

half_log = 0.5 * math.log(2.0 * math.pi)

Z_STEPS = (1, 2, 4)
BIT_VALUE = {3: 2 * Z_STEPS[0], 2: 2 * Z_STEPS[1], 1: 2 * Z_STEPS[2], 0: 1}


def spread_of(p):
    value = 0
    for bit, mask in BIT_VALUE.items():
        if p >> bit & 1:
            value ^= mask
    return value


SPREAD = [spread_of(p) for p in range(CB)]
PLACE = [SPREAD.index(v) for v in range(CB)]


def swap(value, axis, by):
    count = lax.axis_size(axis)
    return lax.ppermute(value, axis, [(i, i ^ by) for i in range(count)])


def swap_both(value):
    pairs = [(i, 3 - i) for i in range(4)]
    return lax.ppermute(value, ("loop", "group"), pairs)


def score_kernel(flags, x0, x1, x2, x3, at, means, log_weights, s_out, ms_out, xt_out, diag):
    step = pl.program_id(0)
    per = at.shape[0]

    @pl.when(step == 0)
    def _():
        for shard, ref in enumerate((x0, x1, x2, x3)):
            for part in range(SH // D):
                piece = ref[part * D : (part + 1) * D, :].astype(jnp.float32)
                start = shard * SH + part * D
                xt_out[:, start : start + D] = piece.T.astype(jnp.bfloat16)

    row = lax.broadcasted_iota(jnp.int32, (D, D), 0)
    col = lax.broadcasted_iota(jnp.int32, (D, D), 1)
    base = pl.multiple_of(step * per, per)
    mean_rows = means[pl.ds(base, per), :]
    centres = []
    diagonals = []
    for c in range(per):
        wide = at[c].astype(jnp.float32)
        centres.append(jnp.sum(wide * mean_rows[c : c + 1, :], axis=1, keepdims=True))
        diagonals.append(jnp.sum(jnp.where(row == col, wide, 0.0), axis=0, keepdims=True))
    diag[pl.ds(base, per), :] = jnp.concatenate(diagonals, axis=0)
    tile = 256
    for start in range(0, NF, tile):
        columns = xt_out[:, start : start + tile]
        sums = []
        for c in range(per):
            product = jnp.dot(at[c], columns, preferred_element_type=jnp.float32)
            shifted = product - centres[c]
            sums.append(jnp.sum(shifted * shifted, axis=0, keepdims=True))
        s_out[pl.ds(base, per), start : start + tile] = jnp.concatenate(sums, axis=0)

    @pl.when(step == pl.num_programs(0) - 1)
    def _():
        logdet = jnp.sum(jnp.log(diag[...]), axis=1, keepdims=True)
        bias = log_weights[...] + logdet - half_log * D
        for start in range(0, NF, D):
            shard, block = start // SH, (start % SH) // D
            pieces = []
            for q in range(KC // CB):
                allowed = flags[((shard // 2) * 4 + block) * 4 + q]
                part = s_out[q * CB : (q + 1) * CB, start : start + D]
                score = bias[q * CB : (q + 1) * CB, :] - 0.5 * part
                pieces.append(jnp.where(allowed > 0, score, -jnp.inf))
            masked = jnp.concatenate(pieces, axis=0)
            s_out[:, start : start + D] = masked
            highest = jnp.max(masked, axis=0, keepdims=True)
            ms_out[0:1, start : start + D] = highest
            ms_out[1:2, start : start + D] = jnp.sum(jnp.exp(masked - highest), axis=0, keepdims=True)


def scores_of(flags, shards, at, means, log_weights):
    per = 8
    whole = lambda shape: pl.BlockSpec(shape, lambda i, f: (0,) * len(shape))
    return pl.pallas_call(
        score_kernel,
        out_shape=(
            jax.ShapeDtypeStruct((KC, NF), jnp.float32),
            jax.ShapeDtypeStruct((2, NF), jnp.float32),
            jax.ShapeDtypeStruct((D, NF), jnp.bfloat16),
        ),
        grid_spec=pltpu.PrefetchScalarGridSpec(
            num_scalar_prefetch=1,
            grid=(KC // per,),
            in_specs=[whole((SH, D))] * 4
            + [pl.BlockSpec((per, D, D), lambda i, f: (i, 0, 0)), whole((KC, D)), whole((KC, 1))],
            out_specs=[whole((KC, NF)), whole((2, NF)), whole((D, NF))],
            scratch_shapes=[pltpu.VMEM((KC, D), jnp.float32)],
        ),
        cost_estimate=pl.CostEstimate(
            flops=2 * KC * D * D * NF, bytes_accessed=4 << 20, transcendentals=KC * NF
        ),
        name="scores",
    )(flags, *shards, at, means, log_weights)


def log_total(parts, shard):
    rows = []
    for d, ref in enumerate(parts):
        start = (shard ^ d) * SH
        rows.append((ref[0:1, start : start + SH], ref[1:2, start : start + SH]))
    highest = functools.reduce(jnp.maximum, [m for m, _ in rows])
    total = sum(s * jnp.exp(m - highest) for m, s in rows)
    return highest + jnp.log(total)


def split_pair(value):
    high = value.astype(jnp.bfloat16).astype(jnp.float32)
    return high, value - high


def moment_kernel(own, meta, x0, x1, x2, x3, xt, scores, m0, m1, m2, m3, *refs):
    outs, (weights, left) = refs[:-2], refs[-2:]
    packed = outs[0]
    parts = (m0, m1, m2, m3)
    xs = (x0, x1, x2, x3)
    first = jnp.zeros((CB, D), jnp.float32)
    occupancy = jnp.zeros((CB, 1), jnp.float32)
    for shard in range(4):
        span = slice(shard * SH, (shard + 1) * SH)
        loglik = log_total(parts, shard)
        if own and shard == 0:
            outs[1][...] = loglik
        part = jnp.exp(scores[:, span] - loglik).astype(jnp.bfloat16)
        wide = part.astype(jnp.float32)
        weights[:, span] = wide
        occupancy += jnp.sum(wide, axis=1, keepdims=True)
        first += jnp.dot(part, xs[shard][...], preferred_element_type=jnp.float32)
    left_rows = left.shape[1]
    per = left_rows // D
    first_ref, occupancy_ref = outs[-2], outs[-1]
    first_ref[...] = first
    occupancy_ref[...] = jnp.broadcast_to(occupancy, (CB, D))
    row = lax.broadcasted_iota(jnp.int32, (D, D), 0)
    col = lax.broadcasted_iota(jnp.int32, (D, D), 1)
    row_half = lax.broadcasted_iota(jnp.int32, (HALF, D), 0)
    col_half = lax.broadcasted_iota(jnp.int32, (HALF, D), 1)
    keep_top = (col_half >= HALF) | (col_half >= row_half)
    for group in range(CB // per):
        buffer = left.at[group % left.shape[0]]
        places = []
        for c in range(per):
            p = group * per + c
            place = meta[1] ^ SPREAD[p]
            places.append(place)
            line = weights[pl.ds(place, 1), :].astype(jnp.bfloat16)
            buffer[c * D : (c + 1) * D, :] = xt[...] * line
        gram = None
        for shard in range(4):
            term = jnp.dot(
                buffer[:, shard * SH : (shard + 1) * SH],
                xs[shard][...],
                preferred_element_type=jnp.float32,
            )
            gram = term if gram is None else gram + term
        for c in range(per):
            p = group * per + c
            one = gram[c * D : (c + 1) * D, :]
            diagonal = jnp.sum(jnp.where(row == col, one, 0.0), axis=0, keepdims=True)
            moved = pltpu.roll(one[HALF:, :], HALF, 1)
            triangle = jnp.where(keep_top, one[:HALF, :], moved)
            extras = [
                occupancy_ref[pl.ds(places[c], 1), :],
                first_ref[pl.ds(places[c], 1), :],
                diagonal,
            ]
            zero = jnp.zeros((1, D), jnp.float32)
            if own:
                tail = extras + [zero] * 5
            else:
                pairs = [split_pair(v) for v in extras]
                tail = [h for h, _ in pairs] + [l for _, l in pairs] + [zero] * 2
            packed[p, 0:HALF, :] = triangle.astype(packed.dtype)
            packed[p, HALF:ROWS, :] = jnp.concatenate(tail, axis=0).astype(packed.dtype)


def moments_of(chunk, meta, shards, xt, scores, partials):
    own = chunk == 0
    whole = lambda shape: pl.BlockSpec(shape, lambda i, f: (0,) * len(shape))
    out_shape = [jax.ShapeDtypeStruct((CB, ROWS, D), jnp.float32 if own else jnp.bfloat16)]
    out_specs = [whole((CB, ROWS, D))]
    if own:
        out_shape.append(jax.ShapeDtypeStruct((1, SH), jnp.float32))
        out_specs.append(whole((1, SH)))
    result = pl.pallas_call(
        functools.partial(moment_kernel, own),
        out_shape=tuple(out_shape),
        grid_spec=pltpu.PrefetchScalarGridSpec(
            num_scalar_prefetch=1,
            grid=(1,),
            in_specs=[whole((SH, D))] * 4
            + [whole((D, NF)), pl.BlockSpec((CB, NF), lambda i, f: (f[0] ^ chunk, 0))]
            + [whole((2, NF))] * 4,
            out_specs=out_specs,
            scratch_shapes=[
                pltpu.VMEM((CB, D), jnp.float32),
                pltpu.VMEM((CB, D), jnp.float32),
                pltpu.VMEM((CB, NF), jnp.float32),
                pltpu.VMEM((2, 4 * D, NF), jnp.bfloat16),
            ],
        ),
        cost_estimate=pl.CostEstimate(
            flops=2 * CB * D * D * NF, bytes_accessed=2 << 20, transcendentals=CB * NF
        ),
        name="moments_own" if own else "moments",
    )(meta, *shards, xt, scores, *partials)
    return result if own else result[0]


def unpack_kernel(chunk, meta, packed, *refs):
    second, first, occupancy = refs[-3:]
    group = pl.program_id(0)
    row = lax.broadcasted_iota(jnp.int32, (D, D), 0)
    col = lax.broadcasted_iota(jnp.int32, (D, D), 1)
    unit = (row == col).astype(jnp.bfloat16)
    row_half = lax.broadcasted_iota(jnp.int32, (HALF, D), 0)
    col_half = lax.broadcasted_iota(jnp.int32, (HALF, D), 1)
    upper = (col_half >= HALF) | (col_half >= row_half)
    lower = (col_half < HALF) | (col_half - HALF < row_half)
    for c in range(8):
        p = meta[2 + group * 8 + c]
        tile = packed[p, 0:HALF, :]
        extra = packed[p, HALF:ROWS, :].astype(jnp.float32)
        occupancy[c : c + 1, :] = extra[0:1, :] + extra[3:4, :]
        first[c : c + 1, :] = extra[1:2, :] + extra[4:5, :]
        diagonal = extra[2:3, :] + extra[5:6, :]
        turned = lax.dot_general(
            unit, tile, (((1,), (1,)), ((), ())), preferred_element_type=jnp.float32
        )
        wide = tile.astype(jnp.float32)
        both = jnp.concatenate([turned[:HALF, :], wide[:, :HALF]], axis=1)
        top = jnp.where(upper, wide, both)
        other = jnp.concatenate([turned[HALF:, :], wide[:, :HALF]], axis=1)
        mirror = jnp.concatenate([turned[HALF:, :], turned[:HALF, :]], axis=1)
        bottom = jnp.where(lower, other, mirror)
        full = jnp.concatenate([top, bottom], axis=0)
        second[:, c, :] = jnp.where(row == col, diagonal, full)


def unpack(chunk, meta, packed, earlier):
    whole = lambda shape: pl.BlockSpec(shape, lambda i, f: (0,) * len(shape))
    place = lambda i, f: (f[0] ^ chunk) * 2 + i
    return pl.pallas_call(
        functools.partial(unpack_kernel, chunk),
        out_shape=(
            jax.ShapeDtypeStruct((D, KC, D), jnp.float32),
            jax.ShapeDtypeStruct((KC, D), jnp.float32),
            jax.ShapeDtypeStruct((KC, D), jnp.float32),
        ),
        grid_spec=pltpu.PrefetchScalarGridSpec(
            num_scalar_prefetch=1,
            grid=(2,),
            in_specs=[whole((CB, ROWS, D))]
            + [pl.BlockSpec(memory_space=pl.ANY)] * len(earlier),
            out_specs=[
                pl.BlockSpec((D, 8, D), lambda i, f: (0, place(i, f), 0)),
                pl.BlockSpec((8, D), lambda i, f: (place(i, f), 0)),
                pl.BlockSpec((8, D), lambda i, f: (place(i, f), 0)),
            ],
        ),
        input_output_aliases={2 + n: n for n in range(len(earlier))},
        cost_estimate=pl.CostEstimate(
            flops=2 * CB * D * D * HALF, bytes_accessed=2 << 20, transcendentals=0
        ),
        name="unpack",
    )(meta, packed, *earlier)


def per_device(frames, factors, comp_means, log_weights, pair_lists, counts):
    own = frames.reshape(SH, D)
    shards = (own, swap(own, "group", 1), swap(own, "loop", 1), swap_both(own))

    loop_index = lax.axis_index("loop")
    y_index, z_index, x_index = (lax.axis_index(a) for a in ("y", "z", "xh"))
    low = z_index * 2 + x_index

    slots = jnp.arange(4, dtype=jnp.int32)
    in_use = slots < counts[:, 0, :, None]
    hits = (pair_lists[:, 0, :, :, None] == slots) & in_use[..., None]
    listed = jnp.any(hits, axis=2).astype(jnp.int32)
    mine = lax.dynamic_index_in_dim(listed, loop_index, 1, keepdims=False)
    theirs = lax.dynamic_index_in_dim(listed, 1 - loop_index, 1, keepdims=False)
    flags = jnp.concatenate([mine.reshape(-1), swap(theirs, "loop", 1).reshape(-1)])

    spots = jnp.arange(CB, dtype=jnp.int32) ^ low
    place = jnp.zeros_like(spots)
    for bit in range(4):
        place = place ^ (((spots >> bit) & 1) * PLACE[1 << bit])
    meta = jnp.concatenate([jnp.stack([y_index, low]).astype(jnp.int32), place])

    at = jnp.transpose(factors, (1, 2, 0))
    scores, partial, xt = scores_of(
        flags, shards, at, comp_means.astype(jnp.float32), log_weights.astype(jnp.float32)[:, None]
    )
    partials = (partial, swap(partial, "group", 1), swap(partial, "loop", 1), swap_both(partial))

    arrived = []
    for chunk in (1, 2, 3):
        packed = moments_of(chunk, meta, shards, xt, scores, partials)
        arrived.append(swap(packed, "y", chunk))
    total, loglik = moments_of(0, meta, shards, xt, scores, partials)
    for piece in arrived:
        total = total + piece.astype(jnp.float32)

    for step in Z_STEPS:
        half = total.shape[0] // 2
        total = total[:half] + swap(total[half:], "z", step)
    total = total[:1] + swap(total[1:], "xh", 1)

    extras = total[:, HALF : HALF + 3] + total[:, HALF + 3 : HALF + 6]
    high = extras.astype(jnp.bfloat16)
    rest = (extras - high.astype(jnp.float32)).astype(jnp.bfloat16)
    spare = jnp.zeros((1, 2, D), jnp.bfloat16)
    held = jnp.concatenate([total[:, :HALF].astype(jnp.bfloat16), high, rest, spare], axis=1)
    held = jnp.concatenate([held, swap(held, "xh", 1)], axis=0)
    for step in reversed(Z_STEPS):
        held = jnp.concatenate([held, swap(held, "z", step)], axis=0)

    pieces = [held] + [swap(held, "y", chunk) for chunk in (1, 2, 3)]
    outs = ()
    for chunk, piece in enumerate(pieces):
        outs = unpack(chunk, meta, piece, outs)
    second, first, occupancy = outs
    return occupancy[:, 0], first, second, loglik.reshape(4, D)


def solution(mesh):
    rep = mesh.shape["rep"]
    fine = Mesh(
        mesh.devices.reshape(2, 2, rep // 8, 4, 2), ("loop", "group", "z", "y", "xh")
    )
    reps = ("z", "y", "xh")
    return jax.shard_map(
        per_device,
        mesh=fine,
        in_specs=(
            P(("loop",) + reps, "group", None),
            P(None, ("loop", "group"), None),
            P(("loop", "group"), None),
            P(("loop", "group")),
            P(("loop",) + reps, "group", None, None),
            P(("loop",) + reps, "group", None),
        ),
        out_specs=(
            P(("loop", "group")),
            P(("loop", "group"), None),
            P(None, ("loop", "group"), None),
            P(("loop",) + reps, "group"),
        ),
        check_vma=False,
    )
```

time: 856 us -> 143 us (0.17)
  blocking collectives: 376 us -> 0 us
  waiting for transfers between devices: 358 us -> 42.8 us
  Pallas kernels: 0 us -> 49.3 us
  matrix products: 36.5 us -> 0 us
  starting transfers between devices: 0.73 us -> 33.7 us
  other arithmetic: 31 us -> 4.77 us
  local copies, waits for them, and re-layouts: 35.7 us -> 10.8 us
  between operations: 14.4 us -> 0.83 us
    psum x1 -> x0, waiting for transfers between devices: 358 us -> none  [per_device(): lax.psum((occupancy, first_moment, second_moment), 'rep')]
    psum x1 -> x0, blocking collectives: 355 us -> none  [per_device(): lax.psum((occupancy, first_moment, second_moment), 'rep')]
    pallas_call x0 -> x9, Pallas kernels: none -> 49.3 us  [the longest x4 21.1 us: moments_of(): pl.pallas_call(functools.partial(moment_kernel, own), out_shape=tuple(out...]
    ppermute x3 -> x21, waiting for transfers between devices: 0.01 us -> 42.8 us  [the longest x19 41.9 us: swap(): return lax.ppermute(value, axis, [(i, i ^ by) for i in range(count)])]
    dot_general x18 -> x0, matrix products: 36.5 us -> none  [the longest x8 24 us: accumulate(): lax.dot_general(frame_block, weighted.reshape(block_rows, panel_size * fe...]
    ppermute x3 -> x21, starting transfers between devices: 0.69 us -> 33.7 us  [the longest x19 32 us: swap(): return lax.ppermute(value, axis, [(i, i ^ by) for i in range(count)])]
    convert_element_type x25 -> x3, other arithmetic: 26.7 us -> 0.63 us  [the longest x1 0.62 us: per_device(): comp_means.astype(jnp.float32)]
    all_gather x4 -> x0, blocking collectives: 17.4 us -> none  [the longest x2 8.71 us: combined_all(): pieces = jax.tree.map(lambda part: lax.all_gather(part, axis), value)]
  transfers between devices with their start and end apart: 4 -> 21, of which waited for: 1 -> 11; matrix products, arithmetic and copies ran while one was open for 3% -> 7% of each run, Pallas kernels for 0% -> 19%
where the time goes in v1:
time: 143 us; the launch traced here: 142 us
  Pallas kernels  49.3 us (34%)
  waiting for transfers between devices  42.8 us (30%)
  starting transfers between devices  33.7 us (24%)
  local copies, waits for them, and re-layouts  10.8 us (8%)
  other arithmetic  4.77 us (3%)
    ppermute x19, waiting for transfers between devices, swap(): return lax.ppermute(value, axis, [(i, i ^ by) for i in range(count)])  41.9 us
    ppermute x19, starting transfers between devices, swap(): return lax.ppermute(value, axis, [(i, i ^ by) for i in range(count)])  32 us
    pallas_call x4, Pallas kernels, moments_of(): pl.pallas_call(functools.partial(moment_kernel, own), out_shape=tuple(out...  21.1 us
    pallas_call x4, Pallas kernels, unpack(): pl.pallas_call(functools.partial(unpack_kernel, chunk), out_shape=(jax.Sh...  14.3 us
    pallas_call x1, Pallas kernels, scores_of(): pl.pallas_call(score_kernel, out_shape=(jax.ShapeDtypeStruct((KC, NF), jn...  13.9 us
    unnamed x26, local copies, waits for them, and re-layouts  7.64 us
  transfers between devices with their start and end apart: 21, of which 11 were waited for; matrix products, arithmetic and copies ran while one was open for 7% of the time, Pallas kernels for 19%

profile of v1, /device:TPU:4, one launch (start us, length us, event | category | flops | bytes accessed | tf_op | source)
XLA Modules:
  0.0 142.1 jit_solution(6445623093820399761)
XLA Ops:
  0.6 1.3 collective-permute-start
  5.4 4.2 %copy.26 = bf16[128,64,128]{0,2,1:T(8,128)(2,1)} copy(bf16[128,64,128]{2,1,0:T(8,128)(2,1)} %param.7) | data formatting | bytes 4194304 | tf_op args[1]
  12.4 13.9 %scores.1 = (f32[64,2048]{1,0:T(8,128)}, f32[2,2048]{1,0:T(2,128)}, bf16[128,2048]{1,0:T(8,128)(2,1)}) custom-call(s32[32]{0:T(128)} %pad_add_fusion.1.flags, bf16[512,128]{1,0:T(8,128)(2,1)} %bitcast.18, bf16[512,128]{1,0:T(8,128)(2,1)} %copy-done.5, bf16[512,128]{1,0:T(8,128)(2,1)} %copy-done.6, bf16[512,128]{1,0:T(8,128)(2,1)} %copy-done.7, ...), custom_call_target="tpu_custom_call" | custom-call | flops 4294967296 | bytes 4194304 | tf_op jit(solution)/shard_map/scores/pallas_call | solution.py:103
  26.3 1.2 collective-permute-start.4
  29.1 1.2 collective-permute-done.4.m1
  31.7 5.3 %moments.3 = bf16[16,72,128]{2,1,0:T(8,128)(2,1)} custom-call(s32[18]{0:T(128)} %pad_add_fusion.meta, bf16[512,128]{1,0:T(8,128)(2,1)} %bitcast.19, bf16[512,128]{1,0:T(8,128)(2,1)} %copy-done.5, bf16[512,128]{1,0:T(8,128)(2,1)} %copy-done.6, bf16[512,128]{1,0:T(8,128)(2,1)} %copy-done.7, bf16[128,2048]{1,0:T(8,128)(2,1)} %get-tuple-element.21.xt, ...), custom_call_target="tpu_custom_call" | custom-call | flops 1073741824 | bytes 2097152 | tf_op jit(solution)/shard_map/moments/pallas_call | solution.py:213
  36.9 1.6 %collective-permute-start.7 = (bf16[16,72,128]{2,1,0:T(8,128)(2,1)}, bf16[16,72,128]{2,1,0:T(8,128)(2,1)S(1)}, u32[]{:S(2)}, u32[]{:S(2)}) collective-permute-start(bf16[16,72,128]{2,1,0:T(8,128)(2,1)} %moments.3), channel_id=1, source_target_pairs={{0,2},{2,0},{4,6},{6,4},{1,3},{3,1},{5,7},{7,5},{8,10},{10,8},{12,... | collective-permute-start | bytes 884744 | tf_op jit(solution)/shard_map/ppermute | solution.py:40
  38.5 5.3 %moments.4 = bf16[16,72,128]{2,1,0:T(8,128)(2,1)} custom-call(s32[18]{0:T(128)} %pad_add_fusion.meta, bf16[512,128]{1,0:T(8,128)(2,1)} %bitcast.20, bf16[512,128]{1,0:T(8,128)(2,1)} %copy-done.5, bf16[512,128]{1,0:T(8,128)(2,1)} %copy-done.6, bf16[512,128]{1,0:T(8,128)(2,1)} %copy-done.7, bf16[128,2048]{1,0:T(8,128)(2,1)} %get-tuple-element.21.xt, ...), custom_call_target="tpu_custom_call" | custom-call | flops 1073741824 | bytes 2097152 | tf_op jit(solution)/shard_map/moments/pallas_call | solution.py:213
  43.7 2.9 %collective-permute-start.8 = (bf16[16,72,128]{2,1,0:T(8,128)(2,1)}, bf16[16,72,128]{2,1,0:T(8,128)(2,1)S(1)}, u32[]{:S(2)}, u32[]{:S(2)}) collective-permute-start(bf16[16,72,128]{2,1,0:T(8,128)(2,1)} %moments.4), channel_id=1, source_target_pairs={{0,4},{2,6},{4,0},{6,2},{1,5},{3,7},{5,1},{7,3},{8,12},{10,14},{12... | collective-permute-start | bytes 884744 | tf_op jit(solution)/shard_map/ppermute | solution.py:40
  46.7 5.2 %moments.5 = bf16[16,72,128]{2,1,0:T(8,128)(2,1)} custom-call(s32[18]{0:T(128)} %pad_add_fusion.meta, bf16[512,128]{1,0:T(8,128)(2,1)} %bitcast.21, bf16[512,128]{1,0:T(8,128)(2,1)} %copy-done.5, bf16[512,128]{1,0:T(8,128)(2,1)} %copy-done.6, bf16[512,128]{1,0:T(8,128)(2,1)} %copy-done.7, bf16[128,2048]{1,0:T(8,128)(2,1)} %get-tuple-element.21.xt, ...), custom_call_target="tpu_custom_call" | custom-call | flops 1073741824 | bytes 2097152 | tf_op jit(solution)/shard_map/moments/pallas_call | solution.py:213
  52.1 5.4 %moments_own.1 = (f32[16,72,128]{2,1,0:T(8,128)}, f32[1,512]{1,0:T(1,128)}) custom-call(s32[18]{0:T(128)} %pad_add_fusion.meta, bf16[512,128]{1,0:T(8,128)(2,1)} %bitcast.22, bf16[512,128]{1,0:T(8,128)(2,1)} %copy-done.5, bf16[512,128]{1,0:T(8,128)(2,1)} %copy-done.6, bf16[512,128]{1,0:T(8,128)(2,1)} %copy-done.7, bf16[128,2048]{1,0:T(8,128)(2,1)} %get-tuple-element.21.xt, ...), custom_call_target="tpu_custom_call" | custom-call | flops 1073741824 | bytes 2097152 | tf_op jit(solution)/shard_map/moments_own/pallas_call | solution.py:213
  57.5 4.5 %collective-permute-done.9 = bf16[16,72,128]{2,1,0:T(8,128)(2,1)S(1)} collective-permute-done((bf16[16,72,128]{2,1,0:T(8,128)(2,1)}, bf16[16,72,128]{2,1,0:T(8,128)(2,1)S(1)}, u32[]{:S(2)}, u32[]{:S(2)}) %collective-permute-start.9) | collective-permute-done | bytes 294944 | tf_op jit(solution)/shard_map/ppermute | solution.py:40
  62.0 1.2 convert_add_fusion
  63.2 2.0 %collective-permute-start.10 = (f32[8,72,128]{2,1,0:T(8,128)S(1)}, f32[8,72,128]{2,1,0:T(8,128)S(1)}, u32[]{:S(2)}, u32[]{:S(2)}) collective-permute-start(f32[8,72,128]{2,1,0:T(8,128)S(1)} %slice.50), channel_id=1, source_target_pairs={{0,8},{8,0},{16,24},{24,16},{32,40},{40,32},{48,56},{56,48},{1,9},... | collective-permute-start | bytes 884744 | tf_op jit(solution)/shard_map/ppermute | solution.py:40
  65.2 6.0 %collective-permute-done.10 = f32[8,72,128]{2,1,0:T(8,128)S(1)} collective-permute-done((f32[8,72,128]{2,1,0:T(8,128)S(1)}, f32[8,72,128]{2,1,0:T(8,128)S(1)}, u32[]{:S(2)}, u32[]{:S(2)}) %collective-permute-start.10) | collective-permute-done | bytes 294944 | tf_op jit(solution)/shard_map/ppermute | solution.py:40
  71.3 3.3 %collective-permute-start.11 = (f32[4,72,128]{2,1,0:T(8,128)S(1)}, f32[4,72,128]{2,1,0:T(8,128)S(1)}, u32[]{:S(2)}, u32[]{:S(2)}) collective-permute-start(f32[4,72,128]{2,1,0:T(8,128)S(1)} %slice.52), channel_id=1, source_target_pairs={{0,16},{8,24},{16,0},{24,8},{32,48},{40,56},{48,32},{56,40},{1,17}... | collective-permute-start | bytes 442376 | tf_op jit(solution)/shard_map/ppermute | solution.py:40
  74.7 5.4 %collective-permute-done.11 = f32[4,72,128]{2,1,0:T(8,128)S(1)} collective-permute-done((f32[4,72,128]{2,1,0:T(8,128)S(1)}, f32[4,72,128]{2,1,0:T(8,128)S(1)}, u32[]{:S(2)}, u32[]{:S(2)}) %collective-permute-start.11) | collective-permute-done | bytes 147488 | tf_op jit(solution)/shard_map/ppermute | solution.py:40
  80.0 6.3 %collective-permute-start.12 = (f32[2,72,128]{2,1,0:T(8,128)S(1)}, f32[2,72,128]{2,1,0:T(8,128)S(1)}, u32[]{:S(2)}, u32[]{:S(2)}) collective-permute-start(f32[2,72,128]{2,1,0:T(8,128)S(1)} %slice.54), channel_id=1, source_target_pairs={{0,32},{8,40},{16,48},{24,56},{32,0},{40,8},{48,16},{56,24},{1,33}... | collective-permute-start | bytes 221192 | tf_op jit(solution)/shard_map/ppermute | solution.py:40
  86.4 2.3 %collective-permute-done.12 = f32[2,72,128]{2,1,0:T(8,128)S(1)} collective-permute-done((f32[2,72,128]{2,1,0:T(8,128)S(1)}, f32[2,72,128]{2,1,0:T(8,128)S(1)}, u32[]{:S(2)}, u32[]{:S(2)}) %collective-permute-start.12) | collective-permute-done | bytes 73760 | tf_op jit(solution)/shard_map/ppermute | solution.py:40
  89.7 4.7 %collective-permute-done.13 = f32[1,72,128]{2,1,0:T(8,128)S(1)} collective-permute-done((f32[1,72,128]{2,1,0:T(8,128)S(1)}, f32[1,72,128]{2,1,0:T(8,128)S(1)}, u32[]{:S(2)}, u32[]{:S(2)}) %collective-permute-start.13) | collective-permute-done | bytes 36896 | tf_op jit(solution)/shard_map/ppermute | solution.py:40
  95.3 4.5 %collective-permute-done.14 = bf16[1,72,128]{2,1,0:T(8,128)(2,1)S(1)} collective-permute-done((bf16[1,72,128]{2,1,0:T(8,128)(2,1)S(1)}, bf16[1,72,128]{2,1,0:T(8,128)(2,1)S(1)}, u32[]{:S(2)}, u32[]{:S(2)}) %collective-permute-start.14) | collective-permute-done | bytes 18464 | tf_op jit(solution)/shard_map/ppermute | solution.py:40
  99.7 6.0 %collective-permute-start.15 = (bf16[2,72,128]{2,1,0:T(8,128)(2,1)S(1)}, bf16[2,72,128]{2,1,0:T(8,128)(2,1)S(1)}, u32[]{:S(2)}, u32[]{:S(2)}) collective-permute-start(bf16[2,72,128]{2,1,0:T(8,128)(2,1)S(1)} %pad_maximum_fusion.2), channel_id=1, source_target_pairs={{0,32},{8,40},{16,48},{24,56},{32,0},{40,8},{48,16},{56,24},{1,33}... | collective-permute-start | bytes 110600 | tf_op jit(solution)/shard_map/ppermute | solution.py:40
  105.7 2.3 %collective-permute-done.15 = bf16[2,72,128]{2,1,0:T(8,128)(2,1)S(1)} collective-permute-done((bf16[2,72,128]{2,1,0:T(8,128)(2,1)S(1)}, bf16[2,72,128]{2,1,0:T(8,128)(2,1)S(1)}, u32[]{:S(2)}, u32[]{:S(2)}) %collective-permute-start.15) | collective-permute-done | bytes 36896 | tf_op jit(solution)/shard_map/ppermute | solution.py:40
  108.2 6.0 %collective-permute-done.16 = bf16[4,72,128]{2,1,0:T(8,128)(2,1)S(1)} collective-permute-done((bf16[4,72,128]{2,1,0:T(8,128)(2,1)S(1)}, bf16[4,72,128]{2,1,0:T(8,128)(2,1)S(1)}, u32[]{:S(2)}, u32[]{:S(2)}) %collective-permute-start.16) | collective-permute-done | bytes 73760 | tf_op jit(solution)/shard_map/ppermute | solution.py:40
  114.4 5.1 %collective-permute-done.17 = bf16[8,72,128]{2,1,0:T(8,128)(2,1)S(1)} collective-permute-done((bf16[8,72,128]{2,1,0:T(8,128)(2,1)S(1)}, bf16[8,72,128]{2,1,0:T(8,128)(2,1)S(1)}, u32[]{:S(2)}, u32[]{:S(2)}) %collective-permute-start.17) | collective-permute-done | bytes 147488 | tf_op jit(solution)/shard_map/ppermute | solution.py:40
  119.5 1.1 collective-permute-start.20
  120.6 2.9 %collective-permute-start.19 = (bf16[16,72,128]{2,1,0:T(8,128)(2,1)S(1)}, bf16[16,72,128]{2,1,0:T(8,128)(2,1)S(1)}, u32[]{:S(2)}, u32[]{:S(2)}) collective-permute-start(bf16[16,72,128]{2,1,0:T(8,128)(2,1)S(1)} %constant_dynamic-update-slice_fusion.packed), channel_id=1, source_target_pairs={{0,4},{2,6},{4,0},{6,2},{1,5},{3,7},{5,1},{7,3},{8,12},{10,14},{12... | collective-permute-start | bytes 884744 | tf_op jit(solution)/shard_map/ppermute | solution.py:40
  124.3 3.6 %unpack.4 = (f32[128,64,128]{2,1,0:T(8,128)}, f32[64,128]{1,0:T(8,128)}, f32[64,128]{1,0:T(8,128)}) custom-call(s32[18]{0:T(128)} %pad_add_fusion.meta, bf16[16,72,128]{2,1,0:T(8,128)(2,1)} %copy-done), custom_call_target="tpu_custom_call" | custom-call | flops 33554432 | bytes 2097152 | tf_op jit(solution)/shard_map/unpack/pallas_call | solution.py:271
  128.6 3.6 %unpack.5 = (f32[128,64,128]{2,1,0:T(8,128)}, f32[64,128]{1,0:T(8,128)}, f32[64,128]{1,0:T(8,128)}) custom-call(s32[18]{0:T(128)} %pad_add_fusion.meta, bf16[16,72,128]{2,1,0:T(8,128)(2,1)} %copy-done.3, f32[128,64,128]{2,1,0:T(8,128)} %get-tuple-element.25.refs_0_, ...), custom_call_target="tpu_custom_call", output_to_operand_aliasing={{0}: (2, {}), {1}: (3, {}), {2}: (4, {})} | custom-call | flops 33554432 | bytes 2097152 | tf_op jit(solution)/shard_map/unpack/pallas_call | solution.py:271
  132.8 3.6 %unpack.6 = (f32[128,64,128]{2,1,0:T(8,128)}, f32[64,128]{1,0:T(8,128)}, f32[64,128]{1,0:T(8,128)}) custom-call(s32[18]{0:T(128)} %pad_add_fusion.meta, bf16[16,72,128]{2,1,0:T(8,128)(2,1)} %copy-done.2, f32[128,64,128]{2,1,0:T(8,128)} %get-tuple-element.28.refs_0_, ...), custom_call_target="tpu_custom_call", output_to_operand_aliasing={{0}: (2, {}), {1}: (3, {}), {2}: (4, {})} | custom-call | flops 33554432 | bytes 2097152 | tf_op jit(solution)/shard_map/unpack/pallas_call | solution.py:271
  137.1 3.6 %unpack.7 = (f32[128,64,128]{2,1,0:T(8,128)}, f32[64,128]{1,0:T(8,128)}, f32[64,128]{1,0:T(8,128)}) custom-call(s32[18]{0:T(128)} %pad_add_fusion.meta, bf16[16,72,128]{2,1,0:T(8,128)(2,1)} %copy-done.1, f32[128,64,128]{2,1,0:T(8,128)} %get-tuple-element.31.refs_0_, ...), custom_call_target="tpu_custom_call", output_to_operand_aliasing={{0}: (2, {}), {1}: (3, {}), {2}: (4, {})} | custom-call | flops 33554432 | bytes 2097152 | tf_op jit(solution)/shard_map/unpack/pallas_call | solution.py:271
  140.7 1.4 slice_reduce_fusion
  (76 shorter events, 14.6 us)
Async XLA Ops:
  0.6 9.6 %copy-start.4 = (bf16[64,128]{1,0:T(8,128)(2,1)S(1)}, bf16[64,128]{1,0:T(8,128)(2,1)}, u32[]{:S(2)}) copy-start(bf16[64,128]{1,0:T(8,128)(2,1)} %param.8) | copy-start | bytes 49156
  0.6 11.0 %collective-permute-start = (bf16[512,128]{1,0:T(8,128)(2,1)}, bf16[512,128]{1,0:T(8,128)(2,1)S(1)}, u32[]{:S(2)}, u32[]{:S(2)}) collective-permute-start(bf16[512,128]{1,0:T(8,128)(2,1)} %bitcast.15), channel_id=1, source_target_pairs={{0,64},{64,0},{1,65},{65,1},{2,66},{66,2},{3,67},{67,3},{4,68},{68... | collective-permute-start | bytes 393224 | tf_op jit(solution)/shard_map/ppermute | solution.py:40
  1.9 9.7 %collective-permute-start.1 = (bf16[512,128]{1,0:T(8,128)(2,1)}, bf16[512,128]{1,0:T(8,128)(2,1)S(1)}, u32[]{:S(2)}, u32[]{:S(2)}) collective-permute-start(bf16[512,128]{1,0:T(8,128)(2,1)} %bitcast.16), channel_id=1, source_target_pairs={{0,128},{128,0},{1,129},{129,1},{2,130},{130,2},{3,131},{131,3},{4... | collective-permute-start | bytes 393224 | tf_op jit(solution)/shard_map/ppermute | solution.py:40
  1.9 9.7 %collective-permute-start.2 = (bf16[512,128]{1,0:T(8,128)(2,1)}, bf16[512,128]{1,0:T(8,128)(2,1)S(1)}, u32[]{:S(2)}, u32[]{:S(2)}) collective-permute-start(bf16[512,128]{1,0:T(8,128)(2,1)} %bitcast.17), channel_id=1, source_target_pairs={{0,192},{64,128},{128,64},{192,0},{1,193},{65,129},{129,65},{193,1... | collective-permute-start | bytes 393224 | tf_op jit(solution)/shard_map/ppermute | solution.py:45
  4.5 6.4 %collective-permute-start.3 = (s32[4,4]{1,0:T(4,128)S(1)}, s32[4,4]{1,0:T(4,128)S(1)}, u32[]{:S(2)}, u32[]{:S(2)}) collective-permute-start(s32[4,4]{1,0:T(4,128)S(1)} %bitcast.13), channel_id=1, source_target_pairs={{0,128},{128,0},{1,129},{129,1},{2,130},{130,2},{3,131},{131,3},{4... | collective-permute-start | bytes 200 | tf_op jit(solution)/shard_map/ppermute | solution.py:40
  11.6 0.7 copy-start.5
  11.6 0.7 copy-start.6
  11.7 0.7 copy-start.7
  26.3 3.9 %collective-permute-start.4 = (f32[2,2048]{1,0:T(2,128)}, f32[2,2048]{1,0:T(2,128)S(1)}, u32[]{:S(2)}, u32[]{:S(2)}) collective-permute-start(f32[2,2048]{1,0:T(2,128)} %get-tuple-element.23.m0), channel_id=1, source_target_pairs={{0,64},{64,0},{1,65},{65,1},{2,66},{66,2},{3,67},{67,3},{4,68},{68... | collective-permute-start | bytes 49160 | tf_op jit(solution)/shard_map/ppermute | solution.py:40
  27.5 2.8 %collective-permute-start.5 = (f32[2,2048]{1,0:T(2,128)}, f32[2,2048]{1,0:T(2,128)S(1)}, u32[]{:S(2)}, u32[]{:S(2)}) collective-permute-start(f32[2,2048]{1,0:T(2,128)} %get-tuple-element.23.m0), channel_id=1, source_target_pairs={{0,128},{128,0},{1,129},{129,1},{2,130},{130,2},{3,131},{131,3},{4... | collective-permute-start | bytes 49160 | tf_op jit(solution)/shard_map/ppermute | solution.py:40
  27.7 3.4 %collective-permute-start.6 = (f32[2,2048]{1,0:T(2,128)}, f32[2,2048]{1,0:T(2,128)S(1)}, u32[]{:S(2)}, u32[]{:S(2)}) collective-permute-start(f32[2,2048]{1,0:T(2,128)} %get-tuple-element.23.m0), channel_id=1, source_target_pairs={{0,192},{64,128},{128,64},{192,0},{1,193},{65,129},{129,65},{193,1... | collective-permute-start | bytes 49160 | tf_op jit(solution)/shard_map/ppermute | solution.py:45
  30.2 0.8 copy-start.8
  30.2 0.8 copy-start.9
  31.1 0.6 copy-start.10
  36.9 20.6 %collective-permute-start.7 = (bf16[16,72,128]{2,1,0:T(8,128)(2,1)}, bf16[16,72,128]{2,1,0:T(8,128)(2,1)S(1)}, u32[]{:S(2)}, u32[]{:S(2)}) collective-permute-start(bf16[16,72,128]{2,1,0:T(8,128)(2,1)} %moments.3), channel_id=1, source_target_pairs={{0,2},{2,0},{4,6},{6,4},{1,3},{3,1},{5,7},{7,5},{8,10},{10,8},{12,... | collective-permute-start | bytes 884744 | tf_op jit(solution)/shard_map/ppermute | solution.py:40
  43.7 13.7 %collective-permute-start.8 = (bf16[16,72,128]{2,1,0:T(8,128)(2,1)}, bf16[16,72,128]{2,1,0:T(8,128)(2,1)S(1)}, u32[]{:S(2)}, u32[]{:S(2)}) collective-permute-start(bf16[16,72,128]{2,1,0:T(8,128)(2,1)} %moments.4), channel_id=1, source_target_pairs={{0,4},{2,6},{4,0},{6,2},{1,5},{3,7},{5,1},{7,3},{8,12},{10,14},{12... | collective-permute-start | bytes 884744 | tf_op jit(solution)/shard_map/ppermute | solution.py:40
  51.9 10.1 %collective-permute-start.9 = (bf16[16,72,128]{2,1,0:T(8,128)(2,1)}, bf16[16,72,128]{2,1,0:T(8,128)(2,1)S(1)}, u32[]{:S(2)}, u32[]{:S(2)}) collective-permute-start(bf16[16,72,128]{2,1,0:T(8,128)(2,1)} %moments.5), channel_id=1, source_target_pairs={{0,6},{2,4},{4,2},{6,0},{1,7},{3,5},{5,3},{7,1},{8,14},{10,12},{12... | collective-permute-start | bytes 884744 | tf_op jit(solution)/shard_map/ppermute | solution.py:40
  63.2 8.1 %collective-permute-start.10 = (f32[8,72,128]{2,1,0:T(8,128)S(1)}, f32[8,72,128]{2,1,0:T(8,128)S(1)}, u32[]{:S(2)}, u32[]{:S(2)}) collective-permute-start(f32[8,72,128]{2,1,0:T(8,128)S(1)} %slice.50), channel_id=1, source_target_pairs={{0,8},{8,0},{16,24},{24,16},{32,40},{40,32},{48,56},{56,48},{1,9},... | collective-permute-start | bytes 884744 | tf_op jit(solution)/shard_map/ppermute | solution.py:40
  71.3 8.7 %collective-permute-start.11 = (f32[4,72,128]{2,1,0:T(8,128)S(1)}, f32[4,72,128]{2,1,0:T(8,128)S(1)}, u32[]{:S(2)}, u32[]{:S(2)}) collective-permute-start(f32[4,72,128]{2,1,0:T(8,128)S(1)} %slice.52), channel_id=1, source_target_pairs={{0,16},{8,24},{16,0},{24,8},{32,48},{40,56},{48,32},{56,40},{1,17}... | collective-permute-start | bytes 442376 | tf_op jit(solution)/shard_map/ppermute | solution.py:40
  80.0 8.7 %collective-permute-start.12 = (f32[2,72,128]{2,1,0:T(8,128)S(1)}, f32[2,72,128]{2,1,0:T(8,128)S(1)}, u32[]{:S(2)}, u32[]{:S(2)}) collective-permute-start(f32[2,72,128]{2,1,0:T(8,128)S(1)} %slice.54), channel_id=1, source_target_pairs={{0,32},{8,40},{16,48},{24,56},{32,0},{40,8},{48,16},{56,24},{1,33}... | collective-permute-start | bytes 221192 | tf_op jit(solution)/shard_map/ppermute | solution.py:40
  88.8 5.5 %collective-permute-start.13 = (f32[1,72,128]{2,1,0:T(8,128)S(1)}, f32[1,72,128]{2,1,0:T(8,128)S(1)}, u32[]{:S(2)}, u32[]{:S(2)}) collective-permute-start(f32[1,72,128]{2,1,0:T(8,128)S(1)} %slice.56), channel_id=1, source_target_pairs={{0,1},{1,0},{2,3},{3,2},{4,5},{5,4},{6,7},{7,6},{8,9},{9,8},{10,11... | collective-permute-start | bytes 110600 | tf_op jit(solution)/shard_map/ppermute | solution.py:40
  94.4 5.4 %collective-permute-start.14 = (bf16[1,72,128]{2,1,0:T(8,128)(2,1)S(1)}, bf16[1,72,128]{2,1,0:T(8,128)(2,1)S(1)}, u32[]{:S(2)}, u32[]{:S(2)}) collective-permute-start(bf16[1,72,128]{2,1,0:T(8,128)(2,1)S(1)} %get-tuple-element.40), channel_id=1, source_target_pairs={{0,1},{1,0},{2,3},{3,2},{4,5},{5,4},{6,7},{7,6},{8,9},{9,8},{10,11... | collective-permute-start | bytes 55304 | tf_op jit(solution)/shard_map/ppermute | solution.py:40
  99.7 8.3 %collective-permute-start.15 = (bf16[2,72,128]{2,1,0:T(8,128)(2,1)S(1)}, bf16[2,72,128]{2,1,0:T(8,128)(2,1)S(1)}, u32[]{:S(2)}, u32[]{:S(2)}) collective-permute-start(bf16[2,72,128]{2,1,0:T(8,128)(2,1)S(1)} %pad_maximum_fusion.2), channel_id=1, source_target_pairs={{0,32},{8,40},{16,48},{24,56},{32,0},{40,8},{48,16},{56,24},{1,33}... | collective-permute-start | bytes 110600 | tf_op jit(solution)/shard_map/ppermute | solution.py:40
  108.1 6.1 %collective-permute-start.16 = (bf16[4,72,128]{2,1,0:T(8,128)(2,1)S(1)}, bf16[4,72,128]{2,1,0:T(8,128)(2,1)S(1)}, u32[]{:S(2)}, u32[]{:S(2)}) collective-permute-start(bf16[4,72,128]{2,1,0:T(8,128)(2,1)S(1)} %pad_maximum_fusion.1), channel_id=1, source_target_pairs={{0,16},{8,24},{16,0},{24,8},{32,48},{40,56},{48,32},{56,40},{1,17}... | collective-permute-start | bytes 221192 | tf_op jit(solution)/shard_map/ppermute | solution.py:40
  114.2 5.2 %collective-permute-start.17 = (bf16[8,72,128]{2,1,0:T(8,128)(2,1)S(1)}, bf16[8,72,128]{2,1,0:T(8,128)(2,1)S(1)}, u32[]{:S(2)}, u32[]{:S(2)}) collective-permute-start(bf16[8,72,128]{2,1,0:T(8,128)(2,1)S(1)} %pad_maximum_fusion), channel_id=1, source_target_pairs={{0,8},{8,0},{16,24},{24,16},{32,40},{40,32},{48,56},{56,48},{1,9},... | collective-permute-start | bytes 442376 | tf_op jit(solution)/shard_map/ppermute | solution.py:40
  119.5 4.8 %copy-start = (bf16[16,72,128]{2,1,0:T(8,128)(2,1)}, bf16[16,72,128]{2,1,0:T(8,128)(2,1)S(1)}, u32[]{:S(2)}) copy-start(bf16[16,72,128]{2,1,0:T(8,128)(2,1)S(1)} %constant_dynamic-update-slice_fusion.packed) | copy-start | bytes 884740
  119.5 8.4 %collective-permute-start.20 = (bf16[16,72,128]{2,1,0:T(8,128)(2,1)S(1)}, bf16[16,72,128]{2,1,0:T(8,128)(2,1)S(1)}, u32[]{:S(2)}, u32[]{:S(2)}) collective-permute-start(bf16[16,72,128]{2,1,0:T(8,128)(2,1)S(1)} %constant_dynamic-update-slice_fusion.packed), channel_id=1, source_target_pairs={{0,2},{2,0},{4,6},{6,4},{1,3},{3,1},{5,7},{7,5},{8,10},{10,8},{12,... | collective-permute-start | bytes 884744 | tf_op jit(solution)/shard_map/ppermute | solution.py:40
  120.6 11.5 %collective-permute-start.19 = (bf16[16,72,128]{2,1,0:T(8,128)(2,1)S(1)}, bf16[16,72,128]{2,1,0:T(8,128)(2,1)S(1)}, u32[]{:S(2)}, u32[]{:S(2)}) collective-permute-start(bf16[16,72,128]{2,1,0:T(8,128)(2,1)S(1)} %constant_dynamic-update-slice_fusion.packed), channel_id=1, source_target_pairs={{0,4},{2,6},{4,0},{6,2},{1,5},{3,7},{5,1},{7,3},{8,12},{10,14},{12... | collective-permute-start | bytes 884744 | tf_op jit(solution)/shard_map/ppermute | solution.py:40
  123.6 12.9 %collective-permute-start.18 = (bf16[16,72,128]{2,1,0:T(8,128)(2,1)S(1)}, bf16[16,72,128]{2,1,0:T(8,128)(2,1)S(1)}, u32[]{:S(2)}, u32[]{:S(2)}) collective-permute-start(bf16[16,72,128]{2,1,0:T(8,128)(2,1)S(1)} %constant_dynamic-update-slice_fusion.packed), channel_id=1, source_target_pairs={{0,6},{2,4},{4,2},{6,0},{1,7},{3,5},{5,3},{7,1},{8,14},{10,12},{12... | collective-permute-start | bytes 884744 | tf_op jit(solution)/shard_map/ppermute | solution.py:40
  127.9 0.7 copy-start.3
  132.1 0.7 copy-start.2
  136.4 0.7 copy-start.1

commit v2 on v1

--- a/solution.py
+++ b/solution.py
@@ -14,25 +14,17 @@
 CB = 16
 NF = 2048
 SH = 512
+PER = 4
 ROWS = 72
 HALF = 64
 
+LIMIT = pltpu.CompilerParams(vmem_limit_bytes=24 << 20)
+
+SPAN = 240.0
+
 half_log = 0.5 * math.log(2.0 * math.pi)
 
-Z_STEPS = (1, 2, 4)
-BIT_VALUE = {3: 2 * Z_STEPS[0], 2: 2 * Z_STEPS[1], 1: 2 * Z_STEPS[2], 0: 1}
-
-
-def spread_of(p):
-    value = 0
-    for bit, mask in BIT_VALUE.items():
-        if p >> bit & 1:
-            value ^= mask
-    return value
-
-
-SPREAD = [spread_of(p) for p in range(CB)]
-PLACE = [SPREAD.index(v) for v in range(CB)]
+Z_STEPS = (1, 2, 7)
 
 
 def swap(value, axis, by):
@@ -60,7 +52,7 @@
     row = lax.broadcasted_iota(jnp.int32, (D, D), 0)
     col = lax.broadcasted_iota(jnp.int32, (D, D), 1)
     base = pl.multiple_of(step * per, per)
-    mean_rows = means[pl.ds(base, per), :]
+    mean_rows = means[pl.ds(base, per), :].astype(jnp.float32)
     centres = []
     diagonals = []
     for c in range(per):
@@ -72,9 +64,10 @@
     for start in range(0, NF, tile):
         columns = xt_out[:, start : start + tile]
         sums = []
+        stacked = at[...].reshape(per * D, D)
+        products = jnp.dot(stacked, columns, preferred_element_type=jnp.float32)
         for c in range(per):
-            product = jnp.dot(at[c], columns, preferred_element_type=jnp.float32)
-            shifted = product - centres[c]
+            shifted = products[c * D : (c + 1) * D, :] - centres[c]
             sums.append(jnp.sum(shifted * shifted, axis=0, keepdims=True))
         s_out[pl.ds(base, per), start : start + tile] = jnp.concatenate(sums, axis=0)
 
@@ -118,6 +111,7 @@
         cost_estimate=pl.CostEstimate(
             flops=2 * KC * D * D * NF, bytes_accessed=4 << 20, transcendentals=KC * NF
         ),
+        compiler_params=LIMIT,
         name="scores",
     )(flags, *shards, at, means, log_weights)
 
@@ -165,21 +159,15 @@
     col_half = lax.broadcasted_iota(jnp.int32, (HALF, D), 1)
     keep_top = (col_half >= HALF) | (col_half >= row_half)
     for group in range(CB // per):
+        places = [meta[1] ^ (group * per + c) for c in range(per)]
         buffer = left.at[group % left.shape[0]]
-        places = []
         for c in range(per):
-            p = group * per + c
-            place = meta[1] ^ SPREAD[p]
-            places.append(place)
-            line = weights[pl.ds(place, 1), :].astype(jnp.bfloat16)
+            line = weights[pl.ds(places[c], 1), :].astype(jnp.bfloat16)
             buffer[c * D : (c + 1) * D, :] = xt[...] * line
         gram = None
         for shard in range(4):
-            term = jnp.dot(
-                buffer[:, shard * SH : (shard + 1) * SH],
-                xs[shard][...],
-                preferred_element_type=jnp.float32,
-            )
+            part = buffer[:, shard * SH : (shard + 1) * SH]
+            term = jnp.dot(part, xs[shard][...], preferred_element_type=jnp.float32)
             gram = term if gram is None else gram + term
         for c in range(per):
             p = group * per + c
@@ -224,12 +212,13 @@
                 pltpu.VMEM((CB, D), jnp.float32),
                 pltpu.VMEM((CB, D), jnp.float32),
                 pltpu.VMEM((CB, NF), jnp.float32),
-                pltpu.VMEM((2, 4 * D, NF), jnp.bfloat16),
+                pltpu.VMEM((2, PER * D, NF), jnp.bfloat16),
             ],
         ),
         cost_estimate=pl.CostEstimate(
             flops=2 * CB * D * D * NF, bytes_accessed=2 << 20, transcendentals=CB * NF
         ),
+        compiler_params=LIMIT,
         name="moments_own" if own else "moments",
     )(meta, *shards, xt, scores, *partials)
     return result if own else result[0]
@@ -238,6 +227,13 @@
 def unpack_kernel(chunk, meta, packed, *refs):
     second, first, occupancy = refs[-3:]
     group = pl.program_id(0)
+    lane = lax.broadcasted_iota(jnp.int32, (1, D), 1)
+
+    @pl.when(group == 0)
+    def _():
+        occupancy[...] = refs[2][...] if chunk else jnp.zeros((1, D), jnp.float32)
+
+    occupied = occupancy[...]
     row = lax.broadcasted_iota(jnp.int32, (D, D), 0)
     col = lax.broadcasted_iota(jnp.int32, (D, D), 1)
     unit = (row == col).astype(jnp.bfloat16)
@@ -246,12 +242,14 @@
     upper = (col_half >= HALF) | (col_half >= row_half)
     lower = (col_half < HALF) | (col_half - HALF < row_half)
     for c in range(8):
-        p = meta[2 + group * 8 + c]
+        p = meta[1] ^ (group * 8 + c)
         tile = packed[p, 0:HALF, :]
         extra = packed[p, HALF:ROWS, :].astype(jnp.float32)
-        occupancy[c : c + 1, :] = extra[0:1, :] + extra[3:4, :]
+        here = (meta[0] ^ chunk) * CB + group * 8 + c
+        occupied = jnp.where(lane == here, extra[0:1, :] + extra[3:4, :], occupied)
         first[c : c + 1, :] = extra[1:2, :] + extra[4:5, :]
         diagonal = extra[2:3, :] + extra[5:6, :]
+        largest = jnp.max(diagonal, axis=1, keepdims=True) * (1.0 / SPAN)
         turned = lax.dot_general(
             unit, tile, (((1,), (1,)), ((), ())), preferred_element_type=jnp.float32
         )
@@ -262,7 +260,10 @@
         mirror = jnp.concatenate([turned[HALF:, :], turned[:HALF, :]], axis=1)
         bottom = jnp.where(lower, other, mirror)
         full = jnp.concatenate([top, bottom], axis=0)
-        second[:, c, :] = jnp.where(row == col, diagonal, full)
+        size = (jnp.log2(jnp.abs(full)) + SPAN / 2) * largest
+        entry = jnp.where(full < 0, -size, size)
+        second[:, c, :] = jnp.where(row == col, diagonal, entry)
+    occupancy[...] = occupied
 
 
 def unpack(chunk, meta, packed, earlier):
@@ -273,25 +274,42 @@
         out_shape=(
             jax.ShapeDtypeStruct((D, KC, D), jnp.float32),
             jax.ShapeDtypeStruct((KC, D), jnp.float32),
-            jax.ShapeDtypeStruct((KC, D), jnp.float32),
+            jax.ShapeDtypeStruct((1, D), jnp.float32),
         ),
         grid_spec=pltpu.PrefetchScalarGridSpec(
             num_scalar_prefetch=1,
             grid=(2,),
             in_specs=[whole((CB, ROWS, D))]
-            + [pl.BlockSpec(memory_space=pl.ANY)] * len(earlier),
+            + [pl.BlockSpec(memory_space=pl.ANY)] * len(earlier[:2])
+            + [whole((1, D))] * len(earlier[2:]),
             out_specs=[
                 pl.BlockSpec((D, 8, D), lambda i, f: (0, place(i, f), 0)),
                 pl.BlockSpec((8, D), lambda i, f: (place(i, f), 0)),
-                pl.BlockSpec((8, D), lambda i, f: (place(i, f), 0)),
+                whole((1, D)),
             ],
         ),
-        input_output_aliases={2 + n: n for n in range(len(earlier))},
+        input_output_aliases={2 + n: n for n in range(len(earlier[:2]))},
         cost_estimate=pl.CostEstimate(
             flops=2 * CB * D * D * HALF, bytes_accessed=2 << 20, transcendentals=0
         ),
+        compiler_params=LIMIT,
         name="unpack",
     )(meta, packed, *earlier)
+
+
+def packed_pairs(total, coded):
+    extras = total[:, HALF : HALF + 3] + total[:, HALF + 3 : HALF + 6]
+    high = lax.reduce_precision(extras, 8, 7)
+    rest = (extras - high).astype(jnp.bfloat16)
+    high = high.astype(jnp.bfloat16)
+    spare = jnp.zeros((total.shape[0], 2, D), jnp.bfloat16)
+    entries = total[:, :HALF]
+    if coded:
+        largest = jnp.max(extras[:, 2:3], axis=2, keepdims=True)
+        size = jnp.minimum(jnp.abs(entries) / jnp.maximum(largest, 1e-30), 1.02)
+        code = jnp.exp2(SPAN * size - SPAN / 2)
+        entries = jnp.where(entries < 0, -code, code)
+    return jnp.concatenate([entries.astype(jnp.bfloat16), high, rest, spare], axis=1)
 
 
 def per_device(frames, factors, comp_means, log_weights, pair_lists, counts):
@@ -299,8 +317,9 @@
     shards = (own, swap(own, "group", 1), swap(own, "loop", 1), swap_both(own))
 
     loop_index = lax.axis_index("loop")
-    y_index, z_index, x_index = (lax.axis_index(a) for a in ("y", "z", "xh"))
-    low = z_index * 2 + x_index
+    z_index = lax.axis_index("z")
+    top = z_index >> 2
+    low = (((z_index & 1) ^ top) * 8) + ((((z_index >> 1) & 1) ^ top) * 4)
 
     slots = jnp.arange(4, dtype=jnp.int32)
     in_use = slots < counts[:, 0, :, None]
@@ -310,15 +329,11 @@
     theirs = lax.dynamic_index_in_dim(listed, 1 - loop_index, 1, keepdims=False)
     flags = jnp.concatenate([mine.reshape(-1), swap(theirs, "loop", 1).reshape(-1)])
 
-    spots = jnp.arange(CB, dtype=jnp.int32) ^ low
-    place = jnp.zeros_like(spots)
-    for bit in range(4):
-        place = place ^ (((spots >> bit) & 1) * PLACE[1 << bit])
-    meta = jnp.concatenate([jnp.stack([y_index, low]).astype(jnp.int32), place])
+    meta = jnp.stack([lax.axis_index("y"), low]).astype(jnp.int32)
 
     at = jnp.transpose(factors, (1, 2, 0))
     scores, partial, xt = scores_of(
-        flags, shards, at, comp_means.astype(jnp.float32), log_weights.astype(jnp.float32)[:, None]
+        flags, shards, at, comp_means, log_weights.astype(jnp.float32)[:, None]
     )
     partials = (partial, swap(partial, "group", 1), swap(partial, "loop", 1), swap_both(partial))
 
@@ -330,18 +345,14 @@
     for piece in arrived:
         total = total + piece.astype(jnp.float32)
 
-    for step in Z_STEPS:
+    for step in Z_STEPS[:2]:
         half = total.shape[0] // 2
-        total = total[:half] + swap(total[half:], "z", step)
-    total = total[:1] + swap(total[1:], "xh", 1)
-
-    extras = total[:, HALF : HALF + 3] + total[:, HALF + 3 : HALF + 6]
-    high = extras.astype(jnp.bfloat16)
-    rest = (extras - high.astype(jnp.float32)).astype(jnp.bfloat16)
-    spare = jnp.zeros((1, 2, D), jnp.bfloat16)
-    held = jnp.concatenate([total[:, :HALF].astype(jnp.bfloat16), high, rest, spare], axis=1)
-    held = jnp.concatenate([held, swap(held, "xh", 1)], axis=0)
-    for step in reversed(Z_STEPS):
+        total = total[:half] + swap(packed_pairs(total[half:], False), "z", step)
+    total = total + swap(total, "z", Z_STEPS[2])
+    total = total + swap(total, "xh", 1)
+
+    held = packed_pairs(total, True)
+    for step in reversed(Z_STEPS[:2]):
         held = jnp.concatenate([held, swap(held, "z", step)], axis=0)
 
     pieces = [held] + [swap(held, "y", chunk) for chunk in (1, 2, 3)]
@@ -349,7 +360,7 @@
     for chunk, piece in enumerate(pieces):
         outs = unpack(chunk, meta, piece, outs)
     second, first, occupancy = outs
-    return occupancy[:, 0], first, second, loglik.reshape(4, D)
+    return occupancy[0, :KC], first, second, loglik.reshape(4, D)
 
 
 def solution(mesh):

time: 143 us -> 111 us (0.78)
  Pallas kernels: 49.3 us -> 34.9 us
  starting transfers between devices: 33.7 us -> 26.8 us
  local copies, waits for them, and re-layouts: 10.8 us -> 4.99 us
  other arithmetic: 4.77 us -> 2.34 us
  waiting for transfers between devices: 42.8 us -> 40.7 us
    pallas_call x4, Pallas kernels: 21.1 us -> 12.7 us  [moments_of(): pl.pallas_call(functools.partial(moment_kernel, own), out_shape=tuple(out...]
    ppermute x19 -> x17, starting transfers between devices: 32 us -> 25.2 us  [swap(): return lax.ppermute(value, axis, [(i, i ^ by) for i in range(count)])]
    unnamed x26 -> x5, local copies, waits for them, and re-layouts: 7.64 us -> 3.31 us
    pallas_call x4, Pallas kernels: 14.3 us -> 10.8 us  [unpack(): pl.pallas_call(functools.partial(unpack_kernel, chunk), out_shape=(jax.Sh...]
    pallas_call x1, Pallas kernels: 13.9 us -> 11.4 us  [scores_of(): pl.pallas_call(score_kernel, out_shape=(jax.ShapeDtypeStruct((KC, NF), jn...]
    ppermute x19 -> x17, waiting for transfers between devices: 41.9 us -> 39.9 us  [swap(): return lax.ppermute(value, axis, [(i, i ^ by) for i in range(count)])]
  transfers between devices with their start and end apart: 21 -> 19, of which waited for: 11 -> 12; matrix products, arithmetic and copies ran while one was open for 7% -> 6% of each run, Pallas kernels for 19% -> 16%
where the time goes in v2:
time: 111 us
  waiting for transfers between devices  40.7 us (37%)
  Pallas kernels  34.9 us (31%)
  starting transfers between devices  26.8 us (24%)
  local copies, waits for them, and re-layouts  4.99 us (4%)
  other arithmetic  2.34 us (2%)
    ppermute x17, waiting for transfers between devices, swap(): return lax.ppermute(value, axis, [(i, i ^ by) for i in range(count)])  39.9 us
    ppermute x17, starting transfers between devices, swap(): return lax.ppermute(value, axis, [(i, i ^ by) for i in range(count)])  25.2 us
    pallas_call x4, Pallas kernels, moments_of(): pl.pallas_call(functools.partial(moment_kernel, own), out_shape=tuple(out...  12.7 us
    pallas_call x1, Pallas kernels, scores_of(): pl.pallas_call(score_kernel, out_shape=(jax.ShapeDtypeStruct((KC, NF), jn...  11.4 us
    pallas_call x4, Pallas kernels, unpack(): pl.pallas_call(functools.partial(unpack_kernel, chunk), out_shape=(jax.Sh...  10.8 us
    unnamed x5, local copies, waits for them, and re-layouts  3.31 us
  transfers between devices with their start and end apart: 19, of which 12 were waited for; matrix products, arithmetic and copies ran while one was open for 6% of the time, Pallas kernels for 16%

profile of v2, /device:TPU:4, one launch (start us, length us, event | category | flops | bytes accessed | tf_op | source)
XLA Modules:
  0.0 110.7 jit_solution(15437307826968144920)
XLA Ops:
  0.7 1.3 %collective-permute-start = (bf16[512,128]{1,0:T(8,128)(2,1)}, bf16[512,128]{1,0:T(8,128)(2,1)S(1)}, u32[]{:S(2)}, u32[]{:S(2)}) collective-permute-start(bf16[512,128]{1,0:T(8,128)(2,1)} %bitcast.14), channel_id=1, source_target_pairs={{0,64},{64,0},{1,65},{65,1},{2,66},{66,2},{3,67},{67,3},{4,68},{68... | collective-permute-start | bytes 393224 | tf_op jit(solution)/shard_map/ppermute | solution.py:32
  1.9 0.9 collective-permute-start.2
  5.4 3.3 %copy.20 = bf16[128,64,128]{0,2,1:T(8,128)(2,1)S(1)} copy(bf16[128,64,128]{2,1,0:T(8,128)(2,1)} %param.7) | data formatting | bytes 4194304 | tf_op args[1]
  9.0 11.4 %scores.1 = (f32[64,2048]{1,0:T(8,128)S(1)}, f32[2,2048]{1,0:T(2,128)S(1)}, bf16[128,2048]{1,0:T(8,128)(2,1)S(1)}) custom-call(s32[32]{0:T(128)S(1)} %pad_add_fusion.1.flags, bf16[512,128]{1,0:T(8,128)(2,1)S(1)} %bitcast.17, bf16[512,128]{1,0:T(8,128)(2,1)S(1)} %collective-permute-done.x1, bf16[512,128]{1,0:T(8,128)(2,1)S(1)} %collective-permute-done.1.x2, ...), custom_call_target="tpu_custom_call" | custom-call | flops 4294967296 | bytes 4194304 | tf_op jit(solution)/shard_map/scores/pallas_call | solution.py:96
  20.4 1.3 %collective-permute-start.4 = (f32[2,2048]{1,0:T(2,128)S(1)}, f32[2,2048]{1,0:T(2,128)S(1)}, u32[]{:S(2)}, u32[]{:S(2)}) collective-permute-start(f32[2,2048]{1,0:T(2,128)S(1)} %get-tuple-element.23.m0), channel_id=1, source_target_pairs={{0,64},{64,0},{1,65},{65,1},{2,66},{66,2},{3,67},{67,3},{4,68},{68... | collective-permute-start | bytes 49160 | tf_op jit(solution)/shard_map/ppermute | solution.py:32
  22.7 1.5 %collective-permute-done.4.m1 = f32[2,2048]{1,0:T(2,128)S(1)} collective-permute-done((f32[2,2048]{1,0:T(2,128)S(1)}, f32[2,2048]{1,0:T(2,128)S(1)}, u32[]{:S(2)}, u32[]{:S(2)}) %collective-permute-start.4) | collective-permute-done | bytes 16416 | tf_op jit(solution)/shard_map/ppermute | solution.py:32
  24.2 0.8 collective-permute-done.6.m3
  25.0 3.1 %moments.3 = bf16[16,72,128]{2,1,0:T(8,128)(2,1)S(1)} custom-call(s32[2]{0:T(128)S(1)} %pad_add_fusion.meta, bf16[512,128]{1,0:T(8,128)(2,1)S(1)} %bitcast.18, bf16[512,128]{1,0:T(8,128)(2,1)S(1)} %collective-permute-done.x1, bf16[512,128]{1,0:T(8,128)(2,1)S(1)} %collective-permute-done.1.x2, bf16[512,128]{1,0:T(8,128)(2,1)S(1)} %collective-permute-done.2.x3, ...), custom_call_target="tpu_custom_call" | custom-call | flops 1073741824 | bytes 2097152 | tf_op jit(solution)/shard_map/moments/pallas_call | solution.py:201
  28.1 1.7 %collective-permute-start.7 = (bf16[16,72,128]{2,1,0:T(8,128)(2,1)S(1)}, bf16[16,72,128]{2,1,0:T(8,128)(2,1)S(1)}, u32[]{:S(2)}, u32[]{:S(2)}) collective-permute-start(bf16[16,72,128]{2,1,0:T(8,128)(2,1)S(1)} %moments.3), channel_id=1, source_target_pairs={{0,2},{2,0},{4,6},{6,4},{1,3},{3,1},{5,7},{7,5},{8,10},{10,8},{12,... | collective-permute-start | bytes 884744 | tf_op jit(solution)/shard_map/ppermute | solution.py:32
  29.8 3.1 %moments.4 = bf16[16,72,128]{2,1,0:T(8,128)(2,1)S(1)} custom-call(s32[2]{0:T(128)S(1)} %pad_add_fusion.meta, bf16[512,128]{1,0:T(8,128)(2,1)S(1)} %bitcast.19, bf16[512,128]{1,0:T(8,128)(2,1)S(1)} %collective-permute-done.x1, bf16[512,128]{1,0:T(8,128)(2,1)S(1)} %collective-permute-done.1.x2, bf16[512,128]{1,0:T(8,128)(2,1)S(1)} %collective-permute-done.2.x3, ...), custom_call_target="tpu_custom_call" | custom-call | flops 1073741824 | bytes 2097152 | tf_op jit(solution)/shard_map/moments/pallas_call | solution.py:201
  32.8 3.2 %collective-permute-start.8 = (bf16[16,72,128]{2,1,0:T(8,128)(2,1)S(1)}, bf16[16,72,128]{2,1,0:T(8,128)(2,1)S(1)}, u32[]{:S(2)}, u32[]{:S(2)}) collective-permute-start(bf16[16,72,128]{2,1,0:T(8,128)(2,1)S(1)} %moments.4), channel_id=1, source_target_pairs={{0,4},{2,6},{4,0},{6,2},{1,5},{3,7},{5,1},{7,3},{8,12},{10,14},{12... | collective-permute-start | bytes 884744 | tf_op jit(solution)/shard_map/ppermute | solution.py:32
  36.0 3.1 %moments.5 = bf16[16,72,128]{2,1,0:T(8,128)(2,1)S(1)} custom-call(s32[2]{0:T(128)S(1)} %pad_add_fusion.meta, bf16[512,128]{1,0:T(8,128)(2,1)S(1)} %bitcast.20, bf16[512,128]{1,0:T(8,128)(2,1)S(1)} %collective-permute-done.x1, bf16[512,128]{1,0:T(8,128)(2,1)S(1)} %collective-permute-done.1.x2, bf16[512,128]{1,0:T(8,128)(2,1)S(1)} %collective-permute-done.2.x3, ...), custom_call_target="tpu_custom_call" | custom-call | flops 1073741824 | bytes 2097152 | tf_op jit(solution)/shard_map/moments/pallas_call | solution.py:201
  39.4 3.6 %moments_own.1 = (f32[16,72,128]{2,1,0:T(8,128)S(1)}, f32[1,512]{1,0:T(1,128)}) custom-call(s32[2]{0:T(128)S(1)} %pad_add_fusion.meta, bf16[512,128]{1,0:T(8,128)(2,1)S(1)} %bitcast.21, bf16[512,128]{1,0:T(8,128)(2,1)S(1)} %collective-permute-done.x1, bf16[512,128]{1,0:T(8,128)(2,1)S(1)} %collective-permute-done.1.x2, ...), custom_call_target="tpu_custom_call" | custom-call | flops 1073741824 | bytes 2097152 | tf_op jit(solution)/shard_map/moments_own/pallas_call | solution.py:201
  43.0 3.3 %collective-permute-done.8 = bf16[16,72,128]{2,1,0:T(8,128)(2,1)S(1)} collective-permute-done((bf16[16,72,128]{2,1,0:T(8,128)(2,1)S(1)}, bf16[16,72,128]{2,1,0:T(8,128)(2,1)S(1)}, u32[]{:S(2)}, u32[]{:S(2)}) %collective-permute-start.8) | collective-permute-done | bytes 294944 | tf_op jit(solution)/shard_map/ppermute | solution.py:32
  46.3 6.2 %collective-permute-done.9 = bf16[16,72,128]{2,1,0:T(8,128)(2,1)S(1)} collective-permute-done((bf16[16,72,128]{2,1,0:T(8,128)(2,1)S(1)}, bf16[16,72,128]{2,1,0:T(8,128)(2,1)S(1)}, u32[]{:S(2)}, u32[]{:S(2)}) %collective-permute-start.9) | collective-permute-done | bytes 294944 | tf_op jit(solution)/shard_map/ppermute | solution.py:32
  52.8 2.0 %collective-permute-start.10 = (bf16[8,72,128]{2,1,0:T(8,128)(2,1)S(1)}, bf16[8,72,128]{2,1,0:T(8,128)(2,1)S(1)}, u32[]{:S(2)}, u32[]{:S(2)}) collective-permute-start(bf16[8,72,128]{2,1,0:T(8,128)(2,1)S(1)} %maximum_maximum_fusion), channel_id=1, source_target_pairs={{0,8},{8,0},{16,24},{24,16},{32,40},{40,32},{48,56},{56,48},{1,9},... | collective-permute-start | bytes 442376 | tf_op jit(solution)/shard_map/ppermute | solution.py:32
  54.8 4.0 %collective-permute-done.10 = bf16[8,72,128]{2,1,0:T(8,128)(2,1)S(1)} collective-permute-done((bf16[8,72,128]{2,1,0:T(8,128)(2,1)S(1)}, bf16[8,72,128]{2,1,0:T(8,128)(2,1)S(1)}, u32[]{:S(2)}, u32[]{:S(2)}) %collective-permute-start.10) | collective-permute-done | bytes 147488 | tf_op jit(solution)/shard_map/ppermute | solution.py:32
  58.9 3.4 %collective-permute-start.11 = (bf16[4,72,128]{2,1,0:T(8,128)(2,1)S(1)}, bf16[4,72,128]{2,1,0:T(8,128)(2,1)S(1)}, u32[]{:S(2)}, u32[]{:S(2)}) collective-permute-start(bf16[4,72,128]{2,1,0:T(8,128)(2,1)S(1)} %pad_maximum_fusion.3), channel_id=1, source_target_pairs={{0,16},{8,24},{16,0},{24,8},{32,48},{40,56},{48,32},{56,40},{1,17}... | collective-permute-start | bytes 221192 | tf_op jit(solution)/shard_map/ppermute | solution.py:32
  62.3 2.8 %collective-permute-done.11 = bf16[4,72,128]{2,1,0:T(8,128)(2,1)S(1)} collective-permute-done((bf16[4,72,128]{2,1,0:T(8,128)(2,1)S(1)}, bf16[4,72,128]{2,1,0:T(8,128)(2,1)S(1)}, u32[]{:S(2)}, u32[]{:S(2)}) %collective-permute-start.11) | collective-permute-done | bytes 73760 | tf_op jit(solution)/shard_map/ppermute | solution.py:32
  65.1 5.9 %collective-permute-start.12 = (f32[4,72,128]{2,1,0:T(8,128)S(1)}, f32[4,72,128]{2,1,0:T(8,128)S(1)}, u32[]{:S(2)}, u32[]{:S(2)}) collective-permute-start(f32[4,72,128]{2,1,0:T(8,128)S(1)} %slice_add_fusion.1), channel_id=1, source_target_pairs={{0,56},{8,48},{16,40},{24,32},{32,24},{40,16},{48,8},{56,0},{1,57}... | collective-permute-start | bytes 442376 | tf_op jit(solution)/shard_map/ppermute | solution.py:32
  70.9 4.8 %collective-permute-done.12 = f32[4,72,128]{2,1,0:T(8,128)S(1)} collective-permute-done((f32[4,72,128]{2,1,0:T(8,128)S(1)}, f32[4,72,128]{2,1,0:T(8,128)S(1)}, u32[]{:S(2)}, u32[]{:S(2)}) %collective-permute-start.12) | collective-permute-done | bytes 147488 | tf_op jit(solution)/shard_map/ppermute | solution.py:32
  75.8 0.9 collective-permute-start.13
  76.7 5.8 %collective-permute-done.13 = f32[4,72,128]{2,1,0:T(8,128)S(1)} collective-permute-done((f32[4,72,128]{2,1,0:T(8,128)S(1)}, f32[4,72,128]{2,1,0:T(8,128)S(1)}, u32[]{:S(2)}, u32[]{:S(2)}) %collective-permute-start.13) | collective-permute-done | bytes 147488 | tf_op jit(solution)/shard_map/ppermute | solution.py:32
  83.0 5.2 %collective-permute-done.14 = bf16[4,72,128]{2,1,0:T(8,128)(2,1)S(1)} collective-permute-done((bf16[4,72,128]{2,1,0:T(8,128)(2,1)S(1)}, bf16[4,72,128]{2,1,0:T(8,128)(2,1)S(1)}, u32[]{:S(2)}, u32[]{:S(2)}) %collective-permute-start.14) | collective-permute-done | bytes 73760 | tf_op jit(solution)/shard_map/ppermute | solution.py:32
  88.3 5.1 %collective-permute-done.15 = bf16[8,72,128]{2,1,0:T(8,128)(2,1)S(1)} collective-permute-done((bf16[8,72,128]{2,1,0:T(8,128)(2,1)S(1)}, bf16[8,72,128]{2,1,0:T(8,128)(2,1)S(1)}, u32[]{:S(2)}, u32[]{:S(2)}) %collective-permute-start.15) | collective-permute-done | bytes 147488 | tf_op jit(solution)/shard_map/ppermute | solution.py:32
  93.7 1.6 %collective-permute-start.17 = (bf16[16,72,128]{2,1,0:T(8,128)(2,1)S(1)}, bf16[16,72,128]{2,1,0:T(8,128)(2,1)S(1)}, u32[]{:S(2)}, u32[]{:S(2)}) collective-permute-start(bf16[16,72,128]{2,1,0:T(8,128)(2,1)S(1)} %pad_maximum_fusion.packed), channel_id=1, source_target_pairs={{0,4},{2,6},{4,0},{6,2},{1,5},{3,7},{5,1},{7,3},{8,12},{10,14},{12... | collective-permute-start | bytes 884744 | tf_op jit(solution)/shard_map/ppermute | solution.py:32
  95.3 3.0 %collective-permute-start.16 = (bf16[16,72,128]{2,1,0:T(8,128)(2,1)S(1)}, bf16[16,72,128]{2,1,0:T(8,128)(2,1)S(1)}, u32[]{:S(2)}, u32[]{:S(2)}) collective-permute-start(bf16[16,72,128]{2,1,0:T(8,128)(2,1)S(1)} %pad_maximum_fusion.packed), channel_id=1, source_target_pairs={{0,6},{2,4},{4,2},{6,0},{1,7},{3,5},{5,3},{7,1},{8,14},{10,12},{12... | collective-permute-start | bytes 884744 | tf_op jit(solution)/shard_map/ppermute | solution.py:32
  98.3 2.7 %unpack.4 = (f32[128,64,128]{2,1,0:T(8,128)}, f32[64,128]{1,0:T(8,128)}, f32[1,128]{1,0:T(1,128)S(1)}) custom-call(s32[2]{0:T(128)S(1)} %pad_add_fusion.meta, bf16[16,72,128]{2,1,0:T(8,128)(2,1)S(1)} %pad_maximum_fusion.packed), custom_call_target="tpu_custom_call" | custom-call | flops 33554432 | bytes 2097152 | tf_op jit(solution)/shard_map/unpack/pallas_call | solution.py:272
  101.0 0.8 collective-permute-done.18.packed
  101.8 2.7 %unpack.5 = (f32[128,64,128]{2,1,0:T(8,128)}, f32[64,128]{1,0:T(8,128)}, f32[1,128]{1,0:T(1,128)S(1)}) custom-call(s32[2]{0:T(128)S(1)} %pad_add_fusion.meta, bf16[16,72,128]{2,1,0:T(8,128)(2,1)S(1)} %collective-permute-done.18.packed, f32[128,64,128]{2,1,0:T(8,128)} %get-tuple-element.25.refs_0_, ...), custom_call_target="tpu_custom_call", output_to_operand_aliasing={{0}: (2, {}), {1}: (3, {})} | custom-call | flops 33554432 | bytes 2097152 | tf_op jit(solution)/shard_map/unpack/pallas_call | solution.py:272
  104.7 2.7 %unpack.6 = (f32[128,64,128]{2,1,0:T(8,128)}, f32[64,128]{1,0:T(8,128)}, f32[1,128]{1,0:T(1,128)S(1)}) custom-call(s32[2]{0:T(128)S(1)} %pad_add_fusion.meta, bf16[16,72,128]{2,1,0:T(8,128)(2,1)S(1)} %collective-permute-done.17.packed, f32[128,64,128]{2,1,0:T(8,128)} %get-tuple-element.28.refs_0_, ...), custom_call_target="tpu_custom_call", output_to_operand_aliasing={{0}: (2, {}), {1}: (3, {})} | custom-call | flops 33554432 | bytes 2097152 | tf_op jit(solution)/shard_map/unpack/pallas_call | solution.py:272
  107.4 2.7 %unpack.7 = (f32[128,64,128]{2,1,0:T(8,128)}, f32[64,128]{1,0:T(8,128)}, f32[1,128]{1,0:T(1,128)S(1)}) custom-call(s32[2]{0:T(128)S(1)} %pad_add_fusion.meta, bf16[16,72,128]{2,1,0:T(8,128)(2,1)S(1)} %collective-permute-done.16.packed, f32[128,64,128]{2,1,0:T(8,128)} %get-tuple-element.31.refs_0_, ...), custom_call_target="tpu_custom_call", output_to_operand_aliasing={{0}: (2, {}), {1}: (3, {})} | custom-call | flops 33554432 | bytes 2097152 | tf_op jit(solution)/shard_map/unpack/pallas_call | solution.py:272
  (54 shorter events, 6.1 us)
Async XLA Ops:
  0.6 8.4 %copy-start = (bf16[4,128,128]{2,1,0:T(8,128)(2,1)S(1)}, bf16[4,128,128]{2,1,0:T(8,128)(2,1)}, u32[]{:S(2)}) copy-start(bf16[4,128,128]{2,1,0:T(8,128)(2,1)} %param.6) | copy-start | bytes 393220
  0.6 8.4 %copy-start.1 = (bf16[64,128]{1,0:T(8,128)(2,1)S(1)}, bf16[64,128]{1,0:T(8,128)(2,1)}, u32[]{:S(2)}) copy-start(bf16[64,128]{1,0:T(8,128)(2,1)} %means.1) | copy-start | bytes 49156
  0.7 8.3 %collective-permute-start = (bf16[512,128]{1,0:T(8,128)(2,1)}, bf16[512,128]{1,0:T(8,128)(2,1)S(1)}, u32[]{:S(2)}, u32[]{:S(2)}) collective-permute-start(bf16[512,128]{1,0:T(8,128)(2,1)} %bitcast.14), channel_id=1, source_target_pairs={{0,64},{64,0},{1,65},{65,1},{2,66},{66,2},{3,67},{67,3},{4,68},{68... | collective-permute-start | bytes 393224 | tf_op jit(solution)/shard_map/ppermute | solution.py:32
  1.9 7.0 %collective-permute-start.1 = (bf16[512,128]{1,0:T(8,128)(2,1)}, bf16[512,128]{1,0:T(8,128)(2,1)S(1)}, u32[]{:S(2)}, u32[]{:S(2)}) collective-permute-start(bf16[512,128]{1,0:T(8,128)(2,1)} %bitcast.15), channel_id=1, source_target_pairs={{0,128},{128,0},{1,129},{129,1},{2,130},{130,2},{3,131},{131,3},{4... | collective-permute-start | bytes 393224 | tf_op jit(solution)/shard_map/ppermute | solution.py:32
  1.9 7.0 %collective-permute-start.2 = (bf16[512,128]{1,0:T(8,128)(2,1)}, bf16[512,128]{1,0:T(8,128)(2,1)S(1)}, u32[]{:S(2)}, u32[]{:S(2)}) collective-permute-start(bf16[512,128]{1,0:T(8,128)(2,1)} %bitcast.16), channel_id=1, source_target_pairs={{0,192},{64,128},{128,64},{192,0},{1,193},{65,129},{129,65},{193,1... | collective-permute-start | bytes 393224 | tf_op jit(solution)/shard_map/ppermute | solution.py:37
  4.6 4.3 %collective-permute-start.3 = (s32[4,4]{1,0:T(4,128)S(1)}, s32[4,4]{1,0:T(4,128)S(1)}, u32[]{:S(2)}, u32[]{:S(2)}) collective-permute-start(s32[4,4]{1,0:T(4,128)S(1)} %bitcast.23), channel_id=1, source_target_pairs={{0,128},{128,0},{1,129},{129,1},{2,130},{130,2},{3,131},{131,3},{4... | collective-permute-start | bytes 200 | tf_op jit(solution)/shard_map/ppermute | solution.py:32
  20.4 3.8 %collective-permute-start.4 = (f32[2,2048]{1,0:T(2,128)S(1)}, f32[2,2048]{1,0:T(2,128)S(1)}, u32[]{:S(2)}, u32[]{:S(2)}) collective-permute-start(f32[2,2048]{1,0:T(2,128)S(1)} %get-tuple-element.23.m0), channel_id=1, source_target_pairs={{0,64},{64,0},{1,65},{65,1},{2,66},{66,2},{3,67},{67,3},{4,68},{68... | collective-permute-start | bytes 49160 | tf_op jit(solution)/shard_map/ppermute | solution.py:32
  21.7 2.5 %collective-permute-start.5 = (f32[2,2048]{1,0:T(2,128)S(1)}, f32[2,2048]{1,0:T(2,128)S(1)}, u32[]{:S(2)}, u32[]{:S(2)}) collective-permute-start(f32[2,2048]{1,0:T(2,128)S(1)} %get-tuple-element.23.m0), channel_id=1, source_target_pairs={{0,128},{128,0},{1,129},{129,1},{2,130},{130,2},{3,131},{131,3},{4... | collective-permute-start | bytes 49160 | tf_op jit(solution)/shard_map/ppermute | solution.py:32
  21.9 3.2 %collective-permute-start.6 = (f32[2,2048]{1,0:T(2,128)S(1)}, f32[2,2048]{1,0:T(2,128)S(1)}, u32[]{:S(2)}, u32[]{:S(2)}) collective-permute-start(f32[2,2048]{1,0:T(2,128)S(1)} %get-tuple-element.23.m0), channel_id=1, source_target_pairs={{0,192},{64,128},{128,64},{192,0},{1,193},{65,129},{129,65},{193,1... | collective-permute-start | bytes 49160 | tf_op jit(solution)/shard_map/ppermute | solution.py:37
  28.1 14.9 %collective-permute-start.7 = (bf16[16,72,128]{2,1,0:T(8,128)(2,1)S(1)}, bf16[16,72,128]{2,1,0:T(8,128)(2,1)S(1)}, u32[]{:S(2)}, u32[]{:S(2)}) collective-permute-start(bf16[16,72,128]{2,1,0:T(8,128)(2,1)S(1)} %moments.3), channel_id=1, source_target_pairs={{0,2},{2,0},{4,6},{6,4},{1,3},{3,1},{5,7},{7,5},{8,10},{10,8},{12,... | collective-permute-start | bytes 884744 | tf_op jit(solution)/shard_map/ppermute | solution.py:32
  32.8 13.4 %collective-permute-start.8 = (bf16[16,72,128]{2,1,0:T(8,128)(2,1)S(1)}, bf16[16,72,128]{2,1,0:T(8,128)(2,1)S(1)}, u32[]{:S(2)}, u32[]{:S(2)}) collective-permute-start(bf16[16,72,128]{2,1,0:T(8,128)(2,1)S(1)} %moments.4), channel_id=1, source_target_pairs={{0,4},{2,6},{4,0},{6,2},{1,5},{3,7},{5,1},{7,3},{8,12},{10,14},{12... | collective-permute-start | bytes 884744 | tf_op jit(solution)/shard_map/ppermute | solution.py:32
  39.1 13.4 %collective-permute-start.9 = (bf16[16,72,128]{2,1,0:T(8,128)(2,1)S(1)}, bf16[16,72,128]{2,1,0:T(8,128)(2,1)S(1)}, u32[]{:S(2)}, u32[]{:S(2)}) collective-permute-start(bf16[16,72,128]{2,1,0:T(8,128)(2,1)S(1)} %moments.5), channel_id=1, source_target_pairs={{0,6},{2,4},{4,2},{6,0},{1,7},{3,5},{5,3},{7,1},{8,14},{10,12},{12... | collective-permute-start | bytes 884744 | tf_op jit(solution)/shard_map/ppermute | solution.py:32
  52.8 6.0 %collective-permute-start.10 = (bf16[8,72,128]{2,1,0:T(8,128)(2,1)S(1)}, bf16[8,72,128]{2,1,0:T(8,128)(2,1)S(1)}, u32[]{:S(2)}, u32[]{:S(2)}) collective-permute-start(bf16[8,72,128]{2,1,0:T(8,128)(2,1)S(1)} %maximum_maximum_fusion), channel_id=1, source_target_pairs={{0,8},{8,0},{16,24},{24,16},{32,40},{40,32},{48,56},{56,48},{1,9},... | collective-permute-start | bytes 442376 | tf_op jit(solution)/shard_map/ppermute | solution.py:32
  58.9 6.1 %collective-permute-start.11 = (bf16[4,72,128]{2,1,0:T(8,128)(2,1)S(1)}, bf16[4,72,128]{2,1,0:T(8,128)(2,1)S(1)}, u32[]{:S(2)}, u32[]{:S(2)}) collective-permute-start(bf16[4,72,128]{2,1,0:T(8,128)(2,1)S(1)} %pad_maximum_fusion.3), channel_id=1, source_target_pairs={{0,16},{8,24},{16,0},{24,8},{32,48},{40,56},{48,32},{56,40},{1,17}... | collective-permute-start | bytes 221192 | tf_op jit(solution)/shard_map/ppermute | solution.py:32
  65.1 10.7 %collective-permute-start.12 = (f32[4,72,128]{2,1,0:T(8,128)S(1)}, f32[4,72,128]{2,1,0:T(8,128)S(1)}, u32[]{:S(2)}, u32[]{:S(2)}) collective-permute-start(f32[4,72,128]{2,1,0:T(8,128)S(1)} %slice_add_fusion.1), channel_id=1, source_target_pairs={{0,56},{8,48},{16,40},{24,32},{32,24},{40,16},{48,8},{56,0},{1,57}... | collective-permute-start | bytes 442376 | tf_op jit(solution)/shard_map/ppermute | solution.py:32
  75.8 6.7 %collective-permute-start.13 = (f32[4,72,128]{2,1,0:T(8,128)S(1)}, f32[4,72,128]{2,1,0:T(8,128)S(1)}, u32[]{:S(2)}, u32[]{:S(2)}) collective-permute-start(f32[4,72,128]{2,1,0:T(8,128)S(1)} %add.52), channel_id=1, source_target_pairs={{0,1},{1,0},{2,3},{3,2},{4,5},{5,4},{6,7},{7,6},{8,9},{9,8},{10,11... | collective-permute-start | bytes 442376 | tf_op jit(solution)/shard_map/ppermute | solution.py:32
  82.8 5.4 %collective-permute-start.14 = (bf16[4,72,128]{2,1,0:T(8,128)(2,1)S(1)}, bf16[4,72,128]{2,1,0:T(8,128)(2,1)S(1)}, u32[]{:S(2)}, u32[]{:S(2)}) collective-permute-start(bf16[4,72,128]{2,1,0:T(8,128)(2,1)S(1)} %pad_maximum_fusion.2), channel_id=1, source_target_pairs={{0,16},{8,24},{16,0},{24,8},{32,48},{40,56},{48,32},{56,40},{1,17}... | collective-permute-start | bytes 221192 | tf_op jit(solution)/shard_map/ppermute | solution.py:32
  88.2 5.2 %collective-permute-start.15 = (bf16[8,72,128]{2,1,0:T(8,128)(2,1)S(1)}, bf16[8,72,128]{2,1,0:T(8,128)(2,1)S(1)}, u32[]{:S(2)}, u32[]{:S(2)}) collective-permute-start(bf16[8,72,128]{2,1,0:T(8,128)(2,1)S(1)} %pad_maximum_fusion.1), channel_id=1, source_target_pairs={{0,8},{8,0},{16,24},{24,16},{32,40},{40,32},{48,56},{56,48},{1,9},... | collective-permute-start | bytes 442376 | tf_op jit(solution)/shard_map/ppermute | solution.py:32
  93.5 8.3 %collective-permute-start.18 = (bf16[16,72,128]{2,1,0:T(8,128)(2,1)S(1)}, bf16[16,72,128]{2,1,0:T(8,128)(2,1)S(1)}, u32[]{:S(2)}, u32[]{:S(2)}) collective-permute-start(bf16[16,72,128]{2,1,0:T(8,128)(2,1)S(1)} %pad_maximum_fusion.packed), channel_id=1, source_target_pairs={{0,2},{2,0},{4,6},{6,4},{1,3},{3,1},{5,7},{7,5},{8,10},{10,8},{12,... | collective-permute-start | bytes 884744 | tf_op jit(solution)/shard_map/ppermute | solution.py:32
  93.7 11.0 %collective-permute-start.17 = (bf16[16,72,128]{2,1,0:T(8,128)(2,1)S(1)}, bf16[16,72,128]{2,1,0:T(8,128)(2,1)S(1)}, u32[]{:S(2)}, u32[]{:S(2)}) collective-permute-start(bf16[16,72,128]{2,1,0:T(8,128)(2,1)S(1)} %pad_maximum_fusion.packed), channel_id=1, source_target_pairs={{0,4},{2,6},{4,0},{6,2},{1,5},{3,7},{5,1},{7,3},{8,12},{10,14},{12... | collective-permute-start | bytes 884744 | tf_op jit(solution)/shard_map/ppermute | solution.py:32
  95.3 12.2 %collective-permute-start.16 = (bf16[16,72,128]{2,1,0:T(8,128)(2,1)S(1)}, bf16[16,72,128]{2,1,0:T(8,128)(2,1)S(1)}, u32[]{:S(2)}, u32[]{:S(2)}) collective-permute-start(bf16[16,72,128]{2,1,0:T(8,128)(2,1)S(1)} %pad_maximum_fusion.packed), channel_id=1, source_target_pairs={{0,6},{2,4},{4,2},{6,0},{1,7},{3,5},{5,3},{7,1},{8,14},{10,12},{12... | collective-permute-start | bytes 884744 | tf_op jit(solution)/shard_map/ppermute | solution.py:32

commit v3 on v2

--- a/solution.py
+++ b/solution.py
@@ -37,7 +37,7 @@
     return lax.ppermute(value, ("loop", "group"), pairs)
 
 
-def score_kernel(flags, x0, x1, x2, x3, at, means, log_weights, s_out, ms_out, xt_out, diag):
+def score_kernel(panel, list0, list1, size0, size1, x0, x1, x2, x3, at, means, log_weights, s_out, ms_out, xt_out, diag):
     step = pl.program_id(0)
     per = at.shape[0]
 
@@ -74,12 +74,23 @@
     @pl.when(step == pl.num_programs(0) - 1)
     def _():
         logdet = jnp.sum(jnp.log(diag[...]), axis=1, keepdims=True)
-        bias = log_weights[...] + logdet - half_log * D
+        row_k = lax.broadcasted_iota(jnp.int32, (KC, KC), 0)
+        col_k = lax.broadcasted_iota(jnp.int32, (KC, KC), 1)
+        spread = jnp.where(row_k == col_k, log_weights[...].astype(jnp.float32), 0.0)
+        bias = jnp.sum(spread, axis=1, keepdims=True) + logdet - half_log * D
+        listed = []
+        for lists, sizes in ((list0, size0), (list1, size1)):
+            for block in range(4):
+                bits = 0
+                for slot in range(KC // CB):
+                    bit = jnp.left_shift(1, lists[block, 0, panel[0], slot])
+                    bits = bits | jnp.where(slot < sizes[block, 0, panel[0]], bit, 0)
+                listed.append(bits)
         for start in range(0, NF, D):
             shard, block = start // SH, (start % SH) // D
             pieces = []
             for q in range(KC // CB):
-                allowed = flags[((shard // 2) * 4 + block) * 4 + q]
+                allowed = listed[(shard // 2) * 4 + block] & (1 << q)
                 part = s_out[q * CB : (q + 1) * CB, start : start + D]
                 score = bias[q * CB : (q + 1) * CB, :] - 0.5 * part
                 pieces.append(jnp.where(allowed > 0, score, -jnp.inf))
@@ -90,9 +101,9 @@
             ms_out[1:2, start : start + D] = jnp.sum(jnp.exp(masked - highest), axis=0, keepdims=True)
 
 
-def scores_of(flags, shards, at, means, log_weights):
+def scores_of(scalars, shards, at, means, log_weights):
     per = 8
-    whole = lambda shape: pl.BlockSpec(shape, lambda i, f: (0,) * len(shape))
+    whole = lambda shape: pl.BlockSpec(shape, lambda i, *f: (0,) * len(shape))
     return pl.pallas_call(
         score_kernel,
         out_shape=(
@@ -101,10 +112,10 @@
             jax.ShapeDtypeStruct((D, NF), jnp.bfloat16),
         ),
         grid_spec=pltpu.PrefetchScalarGridSpec(
-            num_scalar_prefetch=1,
+            num_scalar_prefetch=5,
             grid=(KC // per,),
             in_specs=[whole((SH, D))] * 4
-            + [pl.BlockSpec((per, D, D), lambda i, f: (i, 0, 0)), whole((KC, D)), whole((KC, 1))],
+            + [pl.BlockSpec((per, D, D), lambda i, *f: (i, 0, 0)), whole((KC, D)), whole((1, KC))],
             out_specs=[whole((KC, NF)), whole((2, NF)), whole((D, NF))],
             scratch_shapes=[pltpu.VMEM((KC, D), jnp.float32)],
         ),
@@ -113,7 +124,7 @@
         ),
         compiler_params=LIMIT,
         name="scores",
-    )(flags, *shards, at, means, log_weights)
+    )(*scalars, *shards, at, means, log_weights)
 
 
 def log_total(parts, shard):
@@ -297,19 +308,63 @@
     )(meta, packed, *earlier)
 
 
-def packed_pairs(total, coded):
+def packed_pairs(total):
     extras = total[:, HALF : HALF + 3] + total[:, HALF + 3 : HALF + 6]
     high = lax.reduce_precision(extras, 8, 7)
     rest = (extras - high).astype(jnp.bfloat16)
     high = high.astype(jnp.bfloat16)
     spare = jnp.zeros((total.shape[0], 2, D), jnp.bfloat16)
-    entries = total[:, :HALF]
-    if coded:
-        largest = jnp.max(extras[:, 2:3], axis=2, keepdims=True)
-        size = jnp.minimum(jnp.abs(entries) / jnp.maximum(largest, 1e-30), 1.02)
-        code = jnp.exp2(SPAN * size - SPAN / 2)
-        entries = jnp.where(entries < 0, -code, code)
-    return jnp.concatenate([entries.astype(jnp.bfloat16), high, rest, spare], axis=1)
+    entries = total[:, :HALF].astype(jnp.bfloat16)
+    return jnp.concatenate([entries, high, rest, spare], axis=1)
+
+
+def decode(tile):
+    wide = tile.astype(jnp.float32)
+    largest = jnp.max(wide[HALF + 2 : HALF + 3] + wide[HALF + 5 : HALF + 6], axis=1, keepdims=True)
+    codes = wide[:HALF]
+    size = (jnp.log2(jnp.abs(codes)) + SPAN / 2) * (largest * (1.0 / SPAN))
+    return jnp.where(codes < 0, -size, size), wide[HALF:]
+
+
+def encode(out, c, entries, tail):
+    extras = tail[0:3] + tail[3:6]
+    high, rest = split_pair(extras)
+    largest = jnp.max(extras[2:3], axis=1, keepdims=True)
+    scale = 1.0 / jnp.maximum(largest, 1e-30)
+    code = jnp.exp2(SPAN * jnp.minimum(jnp.abs(entries) * scale, 1.02) - SPAN / 2)
+    out[c, 0:HALF, :] = jnp.where(entries < 0, -code, code).astype(jnp.bfloat16)
+    rows = [high, rest, jnp.zeros((2, D), jnp.float32)]
+    out[c, HALF:ROWS, :] = jnp.concatenate(rows, axis=0).astype(jnp.bfloat16)
+
+
+def first_code_kernel(own, arrived, out):
+    for c in range(out.shape[0]):
+        total = own[c] + arrived[c].astype(jnp.float32)
+        encode(out, c, total[:HALF], total[HALF:])
+
+
+def next_code_kernel(mine, theirs, out):
+    for c in range(out.shape[0]):
+        one, one_tail = decode(mine[c])
+        two, two_tail = decode(theirs[c])
+        encode(out, c, one + two, one_tail + two_tail)
+
+
+def code_sum(kernel, mine, theirs):
+    size = theirs.size
+    whole = pl.BlockSpec(theirs.shape, lambda i: (0, 0, 0))
+    return pl.pallas_call(
+        kernel,
+        out_shape=jax.ShapeDtypeStruct(theirs.shape, jnp.bfloat16),
+        grid=(1,),
+        in_specs=[whole, whole],
+        out_specs=whole,
+        compiler_params=LIMIT,
+        cost_estimate=pl.CostEstimate(
+            flops=8 * size, bytes_accessed=8 * size, transcendentals=3 * size
+        ),
+        name=kernel.__name__,
+    )(mine, theirs)
 
 
 def per_device(frames, factors, comp_means, log_weights, pair_lists, counts):
@@ -321,37 +376,29 @@
     top = z_index >> 2
     low = (((z_index & 1) ^ top) * 8) + ((((z_index >> 1) & 1) ^ top) * 4)
 
-    slots = jnp.arange(4, dtype=jnp.int32)
-    in_use = slots < counts[:, 0, :, None]
-    hits = (pair_lists[:, 0, :, :, None] == slots) & in_use[..., None]
-    listed = jnp.any(hits, axis=2).astype(jnp.int32)
-    mine = lax.dynamic_index_in_dim(listed, loop_index, 1, keepdims=False)
-    theirs = lax.dynamic_index_in_dim(listed, 1 - loop_index, 1, keepdims=False)
-    flags = jnp.concatenate([mine.reshape(-1), swap(theirs, "loop", 1).reshape(-1)])
-
+    lists = (pair_lists, swap(pair_lists, "loop", 1))
+    sizes = (counts, swap(counts, "loop", 1))
     meta = jnp.stack([lax.axis_index("y"), low]).astype(jnp.int32)
 
     at = jnp.transpose(factors, (1, 2, 0))
     scores, partial, xt = scores_of(
-        flags, shards, at, comp_means, log_weights.astype(jnp.float32)[:, None]
+        (loop_index[None], *lists, *sizes), shards, at, comp_means, log_weights[None, :]
     )
     partials = (partial, swap(partial, "group", 1), swap(partial, "loop", 1), swap_both(partial))
 
     arrived = []
-    for chunk in (1, 2, 3):
+    for chunk in (2, 1, 3):
         packed = moments_of(chunk, meta, shards, xt, scores, partials)
         arrived.append(swap(packed, "y", chunk))
     total, loglik = moments_of(0, meta, shards, xt, scores, partials)
     for piece in arrived:
         total = total + piece.astype(jnp.float32)
 
-    for step in Z_STEPS[:2]:
-        half = total.shape[0] // 2
-        total = total[:half] + swap(packed_pairs(total[half:], False), "z", step)
-    total = total + swap(total, "z", Z_STEPS[2])
-    total = total + swap(total, "xh", 1)
-
-    held = packed_pairs(total, True)
+    total = total[:8] + swap(packed_pairs(total[8:]), "z", Z_STEPS[0])
+    arrived = swap(packed_pairs(total[4:]), "z", Z_STEPS[1])
+    held = code_sum(first_code_kernel, total, arrived)
+    held = code_sum(next_code_kernel, held, swap(held, "z", Z_STEPS[2]))
+    held = code_sum(next_code_kernel, held, swap(held, "xh", 1))
     for step in reversed(Z_STEPS[:2]):
         held = jnp.concatenate([held, swap(held, "z", step)], axis=0)
 

time: 111 us -> 103 us (0.928)
  waiting for transfers between devices: 40.7 us -> 32.5 us
  other arithmetic: 2.34 us -> 0.48 us
  starting transfers between devices: 26.8 us -> 28.6 us
    ppermute x17 -> x18, waiting for transfers between devices: 39.9 us -> 30.9 us  [swap(): return lax.ppermute(value, axis, [(i, i ^ by) for i in range(count)])]
    ppermute x17 -> x18, starting transfers between devices: 25.2 us -> 27.2 us  [swap(): return lax.ppermute(value, axis, [(i, i ^ by) for i in range(count)])]
    unnamed x5 -> x10, local copies, waits for them, and re-layouts: 3.31 us -> 4.08 us
  transfers between devices with their start and end apart: 19 -> 20, of which waited for: 12 -> 12; matrix products, arithmetic and copies ran while one was open for 6% -> 4% of each run, Pallas kernels for 16% -> 17%
where the time goes in v3:
time: 103 us
  Pallas kernels  35.6 us (35%)
  waiting for transfers between devices  32.5 us (32%)
  starting transfers between devices  28.6 us (28%)
  local copies, waits for them, and re-layouts  4.71 us (5%)
    ppermute x18, waiting for transfers between devices, swap(): return lax.ppermute(value, axis, [(i, i ^ by) for i in range(count)])  30.9 us
    ppermute x18, starting transfers between devices, swap(): return lax.ppermute(value, axis, [(i, i ^ by) for i in range(count)])  27.2 us
    pallas_call x4, Pallas kernels, moments_of(): pl.pallas_call(functools.partial(moment_kernel, own), out_shape=tuple(out...  12.7 us
    pallas_call x1, Pallas kernels, scores_of(): pl.pallas_call(score_kernel, out_shape=(jax.ShapeDtypeStruct((KC, NF), jn...  11.5 us
    pallas_call x4, Pallas kernels, unpack(): pl.pallas_call(functools.partial(unpack_kernel, chunk), out_shape=(jax.Sh...  10.8 us
    unnamed x10, local copies, waits for them, and re-layouts  4.08 us
  transfers between devices with their start and end apart: 20, of which 12 were waited for; matrix products, arithmetic and copies ran while one was open for 4% of the time, Pallas kernels for 17%

profile of v3, /device:TPU:4, one launch (start us, length us, event | category | flops | bytes accessed | tf_op | source)
XLA Modules:
  0.0 102.7 jit_solution(9888416853832658958)
XLA Ops:
  0.7 1.3 %collective-permute-start = (bf16[512,128]{1,0:T(8,128)(2,1)}, bf16[512,128]{1,0:T(8,128)(2,1)S(1)}, u32[]{:S(2)}, u32[]{:S(2)}) collective-permute-start(bf16[512,128]{1,0:T(8,128)(2,1)} %bitcast.10), channel_id=1, source_target_pairs={{0,64},{64,0},{1,65},{65,1},{2,66},{66,2},{3,67},{67,3},{4,68},{68... | collective-permute-start | bytes 393224 | tf_op jit(solution)/shard_map/ppermute | solution.py:32
  2.0 0.9 collective-permute-start.2
  4.2 3.3 %copy.17 = bf16[128,64,128]{0,2,1:T(8,128)(2,1)S(1)} copy(bf16[128,64,128]{2,1,0:T(8,128)(2,1)} %param.7) | data formatting | bytes 4194304 | tf_op args[1]
  8.0 11.5 %scores.1 = (f32[64,2048]{1,0:T(8,128)S(1)}, f32[2,2048]{1,0:T(2,128)S(1)}, bf16[128,2048]{1,0:T(8,128)(2,1)S(1)}) custom-call(s32[1]{0:T(128)} %bitcast.3.panel, s32[4,1,2,4]{3,2,1,0:T(2,128)S(1)} %copy-done.2, s32[4,1,2,4]{3,2,1,0:T(2,128)S(1)} %collective-permute-done.3.list1, s32[4,1,2]{2,1,0:T(1,128)S(1)} %copy.18.size0, ...), custom_call_target="tpu_custom_call" | custom-call | flops 4294967296 | bytes 4194304 | tf_op jit(solution)/shard_map/scores/pallas_call | solution.py:107
  19.5 1.2 %collective-permute-start.5 = (f32[2,2048]{1,0:T(2,128)S(1)}, f32[2,2048]{1,0:T(2,128)S(1)}, u32[]{:S(2)}, u32[]{:S(2)}) collective-permute-start(f32[2,2048]{1,0:T(2,128)S(1)} %get-tuple-element.23.m0), channel_id=1, source_target_pairs={{0,64},{64,0},{1,65},{65,1},{2,66},{66,2},{3,67},{67,3},{4,68},{68... | collective-permute-start | bytes 49160 | tf_op jit(solution)/shard_map/ppermute | solution.py:32
  21.9 1.5 %collective-permute-done.5.m1 = f32[2,2048]{1,0:T(2,128)S(1)} collective-permute-done((f32[2,2048]{1,0:T(2,128)S(1)}, f32[2,2048]{1,0:T(2,128)S(1)}, u32[]{:S(2)}, u32[]{:S(2)}) %collective-permute-start.5) | collective-permute-done | bytes 16416 | tf_op jit(solution)/shard_map/ppermute | solution.py:32
  23.4 1.1 %collective-permute-done.7.m3 = f32[2,2048]{1,0:T(2,128)S(1)} collective-permute-done((f32[2,2048]{1,0:T(2,128)S(1)}, f32[2,2048]{1,0:T(2,128)S(1)}, u32[]{:S(2)}, u32[]{:S(2)}) %collective-permute-start.7) | collective-permute-done | bytes 16416 | tf_op jit(solution)/shard_map/ppermute | solution.py:37
  24.6 3.1 %moments.3 = bf16[16,72,128]{2,1,0:T(8,128)(2,1)S(1)} custom-call(s32[2]{0:T(128)S(1)} %pad_add_fusion.meta, bf16[512,128]{1,0:T(8,128)(2,1)S(1)} %bitcast.14, bf16[512,128]{1,0:T(8,128)(2,1)S(1)} %collective-permute-done.x1, bf16[512,128]{1,0:T(8,128)(2,1)S(1)} %collective-permute-done.1.x2, bf16[512,128]{1,0:T(8,128)(2,1)S(1)} %collective-permute-done.2.x3, ...), custom_call_target="tpu_custom_call" | custom-call | flops 1073741824 | bytes 2097152 | tf_op jit(solution)/shard_map/moments/pallas_call | solution.py:212
  27.6 3.3 %collective-permute-start.8 = (bf16[16,72,128]{2,1,0:T(8,128)(2,1)S(1)}, bf16[16,72,128]{2,1,0:T(8,128)(2,1)S(1)}, u32[]{:S(2)}, u32[]{:S(2)}) collective-permute-start(bf16[16,72,128]{2,1,0:T(8,128)(2,1)S(1)} %moments.3), channel_id=1, source_target_pairs={{0,4},{2,6},{4,0},{6,2},{1,5},{3,7},{5,1},{7,3},{8,12},{10,14},{12... | collective-permute-start | bytes 884744 | tf_op jit(solution)/shard_map/ppermute | solution.py:32
  30.9 3.1 %moments.4 = bf16[16,72,128]{2,1,0:T(8,128)(2,1)S(1)} custom-call(s32[2]{0:T(128)S(1)} %pad_add_fusion.meta, bf16[512,128]{1,0:T(8,128)(2,1)S(1)} %bitcast.15, bf16[512,128]{1,0:T(8,128)(2,1)S(1)} %collective-permute-done.x1, bf16[512,128]{1,0:T(8,128)(2,1)S(1)} %collective-permute-done.1.x2, bf16[512,128]{1,0:T(8,128)(2,1)S(1)} %collective-permute-done.2.x3, ...), custom_call_target="tpu_custom_call" | custom-call | flops 1073741824 | bytes 2097152 | tf_op jit(solution)/shard_map/moments/pallas_call | solution.py:212
  34.0 0.9 collective-permute-start.9
  34.9 3.1 %moments.5 = bf16[16,72,128]{2,1,0:T(8,128)(2,1)S(1)} custom-call(s32[2]{0:T(128)S(1)} %pad_add_fusion.meta, bf16[512,128]{1,0:T(8,128)(2,1)S(1)} %bitcast.16, bf16[512,128]{1,0:T(8,128)(2,1)S(1)} %collective-permute-done.x1, bf16[512,128]{1,0:T(8,128)(2,1)S(1)} %collective-permute-done.1.x2, bf16[512,128]{1,0:T(8,128)(2,1)S(1)} %collective-permute-done.2.x3, ...), custom_call_target="tpu_custom_call" | custom-call | flops 1073741824 | bytes 2097152 | tf_op jit(solution)/shard_map/moments/pallas_call | solution.py:212
  38.5 3.6 %moments_own.1 = (f32[16,72,128]{2,1,0:T(8,128)S(1)}, f32[1,512]{1,0:T(1,128)}) custom-call(s32[2]{0:T(128)S(1)} %pad_add_fusion.meta, bf16[512,128]{1,0:T(8,128)(2,1)S(1)} %bitcast.17, bf16[512,128]{1,0:T(8,128)(2,1)S(1)} %collective-permute-done.x1, bf16[512,128]{1,0:T(8,128)(2,1)S(1)} %collective-permute-done.1.x2, ...), custom_call_target="tpu_custom_call" | custom-call | flops 1073741824 | bytes 2097152 | tf_op jit(solution)/shard_map/moments_own/pallas_call | solution.py:212
  42.1 2.8 %collective-permute-done.9 = bf16[16,72,128]{2,1,0:T(8,128)(2,1)S(1)} collective-permute-done((bf16[16,72,128]{2,1,0:T(8,128)(2,1)S(1)}, bf16[16,72,128]{2,1,0:T(8,128)(2,1)S(1)}, u32[]{:S(2)}, u32[]{:S(2)}) %collective-permute-start.9) | collective-permute-done | bytes 294944 | tf_op jit(solution)/shard_map/ppermute | solution.py:32
  44.9 2.8 %collective-permute-done.10 = bf16[16,72,128]{2,1,0:T(8,128)(2,1)S(1)} collective-permute-done((bf16[16,72,128]{2,1,0:T(8,128)(2,1)S(1)}, bf16[16,72,128]{2,1,0:T(8,128)(2,1)S(1)}, u32[]{:S(2)}, u32[]{:S(2)}) %collective-permute-start.10) | collective-permute-done | bytes 294944 | tf_op jit(solution)/shard_map/ppermute | solution.py:32
  48.0 2.0 %collective-permute-start.11 = (bf16[8,72,128]{2,1,0:T(8,128)(2,1)S(1)}, bf16[8,72,128]{2,1,0:T(8,128)(2,1)S(1)}, u32[]{:S(2)}, u32[]{:S(2)}) collective-permute-start(bf16[8,72,128]{2,1,0:T(8,128)(2,1)S(1)} %maximum_maximum_fusion), channel_id=1, source_target_pairs={{0,8},{8,0},{16,24},{24,16},{32,40},{40,32},{48,56},{56,48},{1,9},... | collective-permute-start | bytes 442376 | tf_op jit(solution)/shard_map/ppermute | solution.py:32
  50.0 3.2 %collective-permute-done.11 = bf16[8,72,128]{2,1,0:T(8,128)(2,1)S(1)} collective-permute-done((bf16[8,72,128]{2,1,0:T(8,128)(2,1)S(1)}, bf16[8,72,128]{2,1,0:T(8,128)(2,1)S(1)}, u32[]{:S(2)}, u32[]{:S(2)}) %collective-permute-start.11) | collective-permute-done | bytes 147488 | tf_op jit(solution)/shard_map/ppermute | solution.py:32
  53.4 3.4 %collective-permute-start.12 = (bf16[4,72,128]{2,1,0:T(8,128)(2,1)S(1)}, bf16[4,72,128]{2,1,0:T(8,128)(2,1)S(1)}, u32[]{:S(2)}, u32[]{:S(2)}) collective-permute-start(bf16[4,72,128]{2,1,0:T(8,128)(2,1)S(1)} %maximum_maximum_fusion.1), channel_id=1, source_target_pairs={{0,16},{8,24},{16,0},{24,8},{32,48},{40,56},{48,32},{56,40},{1,17}... | collective-permute-start | bytes 221192 | tf_op jit(solution)/shard_map/ppermute | solution.py:32
  56.7 2.3 %collective-permute-done.12.arrived = bf16[4,72,128]{2,1,0:T(8,128)(2,1)S(1)} collective-permute-done((bf16[4,72,128]{2,1,0:T(8,128)(2,1)S(1)}, bf16[4,72,128]{2,1,0:T(8,128)(2,1)S(1)}, u32[]{:S(2)}, u32[]{:S(2)}) %collective-permute-start.12) | collective-permute-done | bytes 73760 | tf_op jit(solution)/shard_map/ppermute | solution.py:32
  59.2 6.4 %collective-permute-start.13 = (bf16[4,72,128]{2,1,0:T(8,128)(2,1)S(1)}, bf16[4,72,128]{2,1,0:T(8,128)(2,1)S(1)}, u32[]{:S(2)}, u32[]{:S(2)}) collective-permute-start(bf16[4,72,128]{2,1,0:T(8,128)(2,1)S(1)} %first_code_kernel.1.mine), channel_id=1, source_target_pairs={{0,56},{8,48},{16,40},{24,32},{32,24},{40,16},{48,8},{56,0},{1,57}... | collective-permute-start | bytes 221192 | tf_op jit(solution)/shard_map/ppermute | solution.py:32
  65.6 2.9 %collective-permute-done.13.theirs = bf16[4,72,128]{2,1,0:T(8,128)(2,1)S(1)} collective-permute-done((bf16[4,72,128]{2,1,0:T(8,128)(2,1)S(1)}, bf16[4,72,128]{2,1,0:T(8,128)(2,1)S(1)}, u32[]{:S(2)}, u32[]{:S(2)}) %collective-permute-start.13) | collective-permute-done | bytes 73760 | tf_op jit(solution)/shard_map/ppermute | solution.py:32
  68.7 0.9 collective-permute-start.14
  69.5 5.1 %collective-permute-done.14.theirs = bf16[4,72,128]{2,1,0:T(8,128)(2,1)S(1)} collective-permute-done((bf16[4,72,128]{2,1,0:T(8,128)(2,1)S(1)}, bf16[4,72,128]{2,1,0:T(8,128)(2,1)S(1)}, u32[]{:S(2)}, u32[]{:S(2)}) %collective-permute-start.14) | collective-permute-done | bytes 73760 | tf_op jit(solution)/shard_map/ppermute | solution.py:32
  74.8 1.3 %collective-permute-start.15 = (bf16[4,72,128]{2,1,0:T(8,128)(2,1)S(1)}, bf16[4,72,128]{2,1,0:T(8,128)(2,1)S(1)}, u32[]{:S(2)}, u32[]{:S(2)}) collective-permute-start(bf16[4,72,128]{2,1,0:T(8,128)(2,1)S(1)} %next_code_kernel.3), channel_id=1, source_target_pairs={{0,16},{8,24},{16,0},{24,8},{32,48},{40,56},{48,32},{56,40},{1,17}... | collective-permute-start | bytes 221192 | tf_op jit(solution)/shard_map/ppermute | solution.py:32
  76.1 4.8 %collective-permute-done.15 = bf16[4,72,128]{2,1,0:T(8,128)(2,1)S(1)} collective-permute-done((bf16[4,72,128]{2,1,0:T(8,128)(2,1)S(1)}, bf16[4,72,128]{2,1,0:T(8,128)(2,1)S(1)}, u32[]{:S(2)}, u32[]{:S(2)}) %collective-permute-start.15) | collective-permute-done | bytes 73760 | tf_op jit(solution)/shard_map/ppermute | solution.py:32
  81.1 5.1 %collective-permute-done.16 = bf16[8,72,128]{2,1,0:T(8,128)(2,1)S(1)} collective-permute-done((bf16[8,72,128]{2,1,0:T(8,128)(2,1)S(1)}, bf16[8,72,128]{2,1,0:T(8,128)(2,1)S(1)}, u32[]{:S(2)}, u32[]{:S(2)}) %collective-permute-start.16) | collective-permute-done | bytes 147488 | tf_op jit(solution)/shard_map/ppermute | solution.py:32
  86.4 2.0 %collective-permute-start.18 = (bf16[16,72,128]{2,1,0:T(8,128)(2,1)S(1)}, bf16[16,72,128]{2,1,0:T(8,128)(2,1)S(1)}, u32[]{:S(2)}, u32[]{:S(2)}) collective-permute-start(bf16[16,72,128]{2,1,0:T(8,128)(2,1)S(1)} %pad_maximum_fusion.packed), channel_id=1, source_target_pairs={{0,4},{2,6},{4,0},{6,2},{1,5},{3,7},{5,1},{7,3},{8,12},{10,14},{12... | collective-permute-start | bytes 884744 | tf_op jit(solution)/shard_map/ppermute | solution.py:32
  88.4 2.6 %collective-permute-start.17 = (bf16[16,72,128]{2,1,0:T(8,128)(2,1)S(1)}, bf16[16,72,128]{2,1,0:T(8,128)(2,1)S(1)}, u32[]{:S(2)}, u32[]{:S(2)}) collective-permute-start(bf16[16,72,128]{2,1,0:T(8,128)(2,1)S(1)} %pad_maximum_fusion.packed), channel_id=1, source_target_pairs={{0,6},{2,4},{4,2},{6,0},{1,7},{3,5},{5,3},{7,1},{8,14},{10,12},{12... | collective-permute-start | bytes 884744 | tf_op jit(solution)/shard_map/ppermute | solution.py:32
  91.0 2.7 %unpack.4 = (f32[128,64,128]{2,1,0:T(8,128)}, f32[64,128]{1,0:T(8,128)}, f32[1,128]{1,0:T(1,128)S(1)}) custom-call(s32[2]{0:T(128)S(1)} %pad_add_fusion.meta, bf16[16,72,128]{2,1,0:T(8,128)(2,1)S(1)} %pad_maximum_fusion.packed), custom_call_target="tpu_custom_call" | custom-call | flops 33554432 | bytes 2097152 | tf_op jit(solution)/shard_map/unpack/pallas_call | solution.py:283
  93.7 2.7 %unpack.5 = (f32[128,64,128]{2,1,0:T(8,128)}, f32[64,128]{1,0:T(8,128)}, f32[1,128]{1,0:T(1,128)S(1)}) custom-call(s32[2]{0:T(128)S(1)} %pad_add_fusion.meta, bf16[16,72,128]{2,1,0:T(8,128)(2,1)S(1)} %collective-permute-done.19.packed, f32[128,64,128]{2,1,0:T(8,128)} %get-tuple-element.25.refs_0_, ...), custom_call_target="tpu_custom_call", output_to_operand_aliasing={{0}: (2, {}), {1}: (3, {})} | custom-call | flops 33554432 | bytes 2097152 | tf_op jit(solution)/shard_map/unpack/pallas_call | solution.py:283
  96.4 2.7 %unpack.6 = (f32[128,64,128]{2,1,0:T(8,128)}, f32[64,128]{1,0:T(8,128)}, f32[1,128]{1,0:T(1,128)S(1)}) custom-call(s32[2]{0:T(128)S(1)} %pad_add_fusion.meta, bf16[16,72,128]{2,1,0:T(8,128)(2,1)S(1)} %collective-permute-done.18.packed, f32[128,64,128]{2,1,0:T(8,128)} %get-tuple-element.28.refs_0_, ...), custom_call_target="tpu_custom_call", output_to_operand_aliasing={{0}: (2, {}), {1}: (3, {})} | custom-call | flops 33554432 | bytes 2097152 | tf_op jit(solution)/shard_map/unpack/pallas_call | solution.py:283
  99.5 2.7 %unpack.7 = (f32[128,64,128]{2,1,0:T(8,128)}, f32[64,128]{1,0:T(8,128)}, f32[1,128]{1,0:T(1,128)S(1)}) custom-call(s32[2]{0:T(128)S(1)} %pad_add_fusion.meta, bf16[16,72,128]{2,1,0:T(8,128)(2,1)S(1)} %collective-permute-done.17.packed, f32[128,64,128]{2,1,0:T(8,128)} %get-tuple-element.31.refs_0_, ...), custom_call_target="tpu_custom_call", output_to_operand_aliasing={{0}: (2, {}), {1}: (3, {})} | custom-call | flops 33554432 | bytes 2097152 | tf_op jit(solution)/shard_map/unpack/pallas_call | solution.py:283
  (44 shorter events, 5.6 us)
Async XLA Ops:
  0.6 7.3 %copy-start = (bf16[4,128,128]{2,1,0:T(8,128)(2,1)S(1)}, bf16[4,128,128]{2,1,0:T(8,128)(2,1)}, u32[]{:S(2)}) copy-start(bf16[4,128,128]{2,1,0:T(8,128)(2,1)} %param.6) | copy-start | bytes 393220
  0.6 7.3 %copy-start.2 = (s32[4,1,2,4]{3,2,1,0:T(2,128)S(1)}, s32[4,1,2,4]{3,2,1,0:T(2,128)}, u32[]{:S(2)}) copy-start(s32[4,1,2,4]{3,2,1,0:T(2,128)} %list0.1) | copy-start | bytes 388
  0.7 7.3 %copy-start.3 = (bf16[64]{0:T(256)(128)(2,1)S(1)}, bf16[64]{0:T(256)(128)(2,1)}, u32[]{:S(2)}) copy-start(bf16[64]{0:T(256)(128)(2,1)} %param.9) | copy-start | bytes 388
  0.7 7.3 %copy-start.1 = (bf16[64,128]{1,0:T(8,128)(2,1)S(1)}, bf16[64,128]{1,0:T(8,128)(2,1)}, u32[]{:S(2)}) copy-start(bf16[64,128]{1,0:T(8,128)(2,1)} %means.1) | copy-start | bytes 49156
  0.7 6.8 %collective-permute-start = (bf16[512,128]{1,0:T(8,128)(2,1)}, bf16[512,128]{1,0:T(8,128)(2,1)S(1)}, u32[]{:S(2)}, u32[]{:S(2)}) collective-permute-start(bf16[512,128]{1,0:T(8,128)(2,1)} %bitcast.10), channel_id=1, source_target_pairs={{0,64},{64,0},{1,65},{65,1},{2,66},{66,2},{3,67},{67,3},{4,68},{68... | collective-permute-start | bytes 393224 | tf_op jit(solution)/shard_map/ppermute | solution.py:32
  2.0 5.6 %collective-permute-start.1 = (bf16[512,128]{1,0:T(8,128)(2,1)}, bf16[512,128]{1,0:T(8,128)(2,1)S(1)}, u32[]{:S(2)}, u32[]{:S(2)}) collective-permute-start(bf16[512,128]{1,0:T(8,128)(2,1)} %bitcast.11), channel_id=1, source_target_pairs={{0,128},{128,0},{1,129},{129,1},{2,130},{130,2},{3,131},{131,3},{4... | collective-permute-start | bytes 393224 | tf_op jit(solution)/shard_map/ppermute | solution.py:32
  2.0 6.0 %collective-permute-start.2 = (bf16[512,128]{1,0:T(8,128)(2,1)}, bf16[512,128]{1,0:T(8,128)(2,1)S(1)}, u32[]{:S(2)}, u32[]{:S(2)}) collective-permute-start(bf16[512,128]{1,0:T(8,128)(2,1)} %bitcast.12), channel_id=1, source_target_pairs={{0,192},{64,128},{128,64},{192,0},{1,193},{65,129},{129,65},{193,1... | collective-permute-start | bytes 393224 | tf_op jit(solution)/shard_map/ppermute | solution.py:37
  3.7 3.8 %collective-permute-start.4 = (s32[4,1,2]{2,1,0:T(1,128)S(1)}, s32[4,1,2]{2,1,0:T(1,128)S(1)}, u32[]{:S(2)}, u32[]{:S(2)}) collective-permute-start(s32[4,1,2]{2,1,0:T(1,128)S(1)} %copy.18.size0), channel_id=1, source_target_pairs={{0,128},{128,0},{1,129},{129,1},{2,130},{130,2},{3,131},{131,3},{4... | collective-permute-start | bytes 104 | tf_op jit(solution)/shard_map/ppermute | solution.py:32
  3.7 3.8 %collective-permute-start.3 = (s32[4,1,2,4]{3,2,1,0:T(2,128)}, s32[4,1,2,4]{3,2,1,0:T(2,128)S(1)}, u32[]{:S(2)}, u32[]{:S(2)}) collective-permute-start(s32[4,1,2,4]{3,2,1,0:T(2,128)} %list0.1), channel_id=1, source_target_pairs={{0,128},{128,0},{1,129},{129,1},{2,130},{130,2},{3,131},{131,3},{4... | collective-permute-start | bytes 392 | tf_op jit(solution)/shard_map/ppermute | solution.py:32
  19.5 3.9 %collective-permute-start.5 = (f32[2,2048]{1,0:T(2,128)S(1)}, f32[2,2048]{1,0:T(2,128)S(1)}, u32[]{:S(2)}, u32[]{:S(2)}) collective-permute-start(f32[2,2048]{1,0:T(2,128)S(1)} %get-tuple-element.23.m0), channel_id=1, source_target_pairs={{0,64},{64,0},{1,65},{65,1},{2,66},{66,2},{3,67},{67,3},{4,68},{68... | collective-permute-start | bytes 49160 | tf_op jit(solution)/shard_map/ppermute | solution.py:32
  20.7 2.7 %collective-permute-start.6 = (f32[2,2048]{1,0:T(2,128)S(1)}, f32[2,2048]{1,0:T(2,128)S(1)}, u32[]{:S(2)}, u32[]{:S(2)}) collective-permute-start(f32[2,2048]{1,0:T(2,128)S(1)} %get-tuple-element.23.m0), channel_id=1, source_target_pairs={{0,128},{128,0},{1,129},{129,1},{2,130},{130,2},{3,131},{131,3},{4... | collective-permute-start | bytes 49160 | tf_op jit(solution)/shard_map/ppermute | solution.py:32
  21.4 3.2 %collective-permute-start.7 = (f32[2,2048]{1,0:T(2,128)S(1)}, f32[2,2048]{1,0:T(2,128)S(1)}, u32[]{:S(2)}, u32[]{:S(2)}) collective-permute-start(f32[2,2048]{1,0:T(2,128)S(1)} %get-tuple-element.23.m0), channel_id=1, source_target_pairs={{0,192},{64,128},{128,64},{192,0},{1,193},{65,129},{129,65},{193,1... | collective-permute-start | bytes 49160 | tf_op jit(solution)/shard_map/ppermute | solution.py:37
  27.6 14.5 %collective-permute-start.8 = (bf16[16,72,128]{2,1,0:T(8,128)(2,1)S(1)}, bf16[16,72,128]{2,1,0:T(8,128)(2,1)S(1)}, u32[]{:S(2)}, u32[]{:S(2)}) collective-permute-start(bf16[16,72,128]{2,1,0:T(8,128)(2,1)S(1)} %moments.3), channel_id=1, source_target_pairs={{0,4},{2,6},{4,0},{6,2},{1,5},{3,7},{5,1},{7,3},{8,12},{10,14},{12... | collective-permute-start | bytes 884744 | tf_op jit(solution)/shard_map/ppermute | solution.py:32
  34.0 10.9 %collective-permute-start.9 = (bf16[16,72,128]{2,1,0:T(8,128)(2,1)S(1)}, bf16[16,72,128]{2,1,0:T(8,128)(2,1)S(1)}, u32[]{:S(2)}, u32[]{:S(2)}) collective-permute-start(bf16[16,72,128]{2,1,0:T(8,128)(2,1)S(1)} %moments.4), channel_id=1, source_target_pairs={{0,2},{2,0},{4,6},{6,4},{1,3},{3,1},{5,7},{7,5},{8,10},{10,8},{12,... | collective-permute-start | bytes 884744 | tf_op jit(solution)/shard_map/ppermute | solution.py:32
  38.0 9.8 %collective-permute-start.10 = (bf16[16,72,128]{2,1,0:T(8,128)(2,1)S(1)}, bf16[16,72,128]{2,1,0:T(8,128)(2,1)S(1)}, u32[]{:S(2)}, u32[]{:S(2)}) collective-permute-start(bf16[16,72,128]{2,1,0:T(8,128)(2,1)S(1)} %moments.5), channel_id=1, source_target_pairs={{0,6},{2,4},{4,2},{6,0},{1,7},{3,5},{5,3},{7,1},{8,14},{10,12},{12... | collective-permute-start | bytes 884744 | tf_op jit(solution)/shard_map/ppermute | solution.py:32
  48.0 5.2 %collective-permute-start.11 = (bf16[8,72,128]{2,1,0:T(8,128)(2,1)S(1)}, bf16[8,72,128]{2,1,0:T(8,128)(2,1)S(1)}, u32[]{:S(2)}, u32[]{:S(2)}) collective-permute-start(bf16[8,72,128]{2,1,0:T(8,128)(2,1)S(1)} %maximum_maximum_fusion), channel_id=1, source_target_pairs={{0,8},{8,0},{16,24},{24,16},{32,40},{40,32},{48,56},{56,48},{1,9},... | collective-permute-start | bytes 442376 | tf_op jit(solution)/shard_map/ppermute | solution.py:32
  53.4 5.7 %collective-permute-start.12 = (bf16[4,72,128]{2,1,0:T(8,128)(2,1)S(1)}, bf16[4,72,128]{2,1,0:T(8,128)(2,1)S(1)}, u32[]{:S(2)}, u32[]{:S(2)}) collective-permute-start(bf16[4,72,128]{2,1,0:T(8,128)(2,1)S(1)} %maximum_maximum_fusion.1), channel_id=1, source_target_pairs={{0,16},{8,24},{16,0},{24,8},{32,48},{40,56},{48,32},{56,40},{1,17}... | collective-permute-start | bytes 221192 | tf_op jit(solution)/shard_map/ppermute | solution.py:32
  59.2 9.3 %collective-permute-start.13 = (bf16[4,72,128]{2,1,0:T(8,128)(2,1)S(1)}, bf16[4,72,128]{2,1,0:T(8,128)(2,1)S(1)}, u32[]{:S(2)}, u32[]{:S(2)}) collective-permute-start(bf16[4,72,128]{2,1,0:T(8,128)(2,1)S(1)} %first_code_kernel.1.mine), channel_id=1, source_target_pairs={{0,56},{8,48},{16,40},{24,32},{32,24},{40,16},{48,8},{56,0},{1,57}... | collective-permute-start | bytes 221192 | tf_op jit(solution)/shard_map/ppermute | solution.py:32
  68.7 5.9 %collective-permute-start.14 = (bf16[4,72,128]{2,1,0:T(8,128)(2,1)S(1)}, bf16[4,72,128]{2,1,0:T(8,128)(2,1)S(1)}, u32[]{:S(2)}, u32[]{:S(2)}) collective-permute-start(bf16[4,72,128]{2,1,0:T(8,128)(2,1)S(1)} %next_code_kernel.2.mine), channel_id=1, source_target_pairs={{0,1},{1,0},{2,3},{3,2},{4,5},{5,4},{6,7},{7,6},{8,9},{9,8},{10,11... | collective-permute-start | bytes 221192 | tf_op jit(solution)/shard_map/ppermute | solution.py:32
  74.8 6.1 %collective-permute-start.15 = (bf16[4,72,128]{2,1,0:T(8,128)(2,1)S(1)}, bf16[4,72,128]{2,1,0:T(8,128)(2,1)S(1)}, u32[]{:S(2)}, u32[]{:S(2)}) collective-permute-start(bf16[4,72,128]{2,1,0:T(8,128)(2,1)S(1)} %next_code_kernel.3), channel_id=1, source_target_pairs={{0,16},{8,24},{16,0},{24,8},{32,48},{40,56},{48,32},{56,40},{1,17}... | collective-permute-start | bytes 221192 | tf_op jit(solution)/shard_map/ppermute | solution.py:32
  80.9 5.2 %collective-permute-start.16 = (bf16[8,72,128]{2,1,0:T(8,128)(2,1)S(1)}, bf16[8,72,128]{2,1,0:T(8,128)(2,1)S(1)}, u32[]{:S(2)}, u32[]{:S(2)}) collective-permute-start(bf16[8,72,128]{2,1,0:T(8,128)(2,1)S(1)} %pad_maximum_fusion.1), channel_id=1, source_target_pairs={{0,8},{8,0},{16,24},{24,16},{32,40},{40,32},{48,56},{56,48},{1,9},... | collective-permute-start | bytes 442376 | tf_op jit(solution)/shard_map/ppermute | solution.py:32
  86.2 7.5 %collective-permute-start.19 = (bf16[16,72,128]{2,1,0:T(8,128)(2,1)S(1)}, bf16[16,72,128]{2,1,0:T(8,128)(2,1)S(1)}, u32[]{:S(2)}, u32[]{:S(2)}) collective-permute-start(bf16[16,72,128]{2,1,0:T(8,128)(2,1)S(1)} %pad_maximum_fusion.packed), channel_id=1, source_target_pairs={{0,2},{2,0},{4,6},{6,4},{1,3},{3,1},{5,7},{7,5},{8,10},{10,8},{12,... | collective-permute-start | bytes 884744 | tf_op jit(solution)/shard_map/ppermute | solution.py:32
  86.4 10.0 %collective-permute-start.18 = (bf16[16,72,128]{2,1,0:T(8,128)(2,1)S(1)}, bf16[16,72,128]{2,1,0:T(8,128)(2,1)S(1)}, u32[]{:S(2)}, u32[]{:S(2)}) collective-permute-start(bf16[16,72,128]{2,1,0:T(8,128)(2,1)S(1)} %pad_maximum_fusion.packed), channel_id=1, source_target_pairs={{0,4},{2,6},{4,0},{6,2},{1,5},{3,7},{5,1},{7,3},{8,12},{10,14},{12... | collective-permute-start | bytes 884744 | tf_op jit(solution)/shard_map/ppermute | solution.py:32
  88.4 11.0 %collective-permute-start.17 = (bf16[16,72,128]{2,1,0:T(8,128)(2,1)S(1)}, bf16[16,72,128]{2,1,0:T(8,128)(2,1)S(1)}, u32[]{:S(2)}, u32[]{:S(2)}) collective-permute-start(bf16[16,72,128]{2,1,0:T(8,128)(2,1)S(1)} %pad_maximum_fusion.packed), channel_id=1, source_target_pairs={{0,6},{2,4},{4,2},{6,0},{1,7},{3,5},{5,3},{7,1},{8,14},{10,12},{12... | collective-permute-start | bytes 884744 | tf_op jit(solution)/shard_map/ppermute | solution.py:32
